TPU v7x, 32 devices: a whole 2x2x4 slice. The times are simulated.
32 devices in a mesh: row: 4 (over y, x), col: 8 (over z, core).
Axes of the slice: x: 2, y: 2, z: 4, core: 2. Of those that a mesh axis runs over, the one named last changes fastest.
Arguments:
- pivot: float32 [1024, 1024], replicated, may hold values from -1 to 2
- col_panel: float32 [2048, 1024], P('row', 'col'), may hold values from -0.25 to 0.25
- row_panel: float32 [1024, 2048], P('row', 'col'), may hold values from -6 to 6
- trailing: float32 [2048, 2048], P('row', 'col'), may hold values from -6 to 6
Outputs:
- updated: float32 [2048, 2048], P('row', 'col')
All inputs are finite; a program needn't handle non-finite values.
Results may differ from a plain program's by a relative error of at most 0.000061.
Values sent between devices are 32-bit elements; how exact they have to be, the bound alone decides.
No kernel may reach another device: no remote copies, remote signals or barrier semaphores. Data moves between devices by JAX's collectives and lax.ppermute only.
A program may use at most 64 MiB of HBM per device.

v0:
```python
import jax
import jax.numpy as jnp
from jax import lax
from jax.sharding import PartitionSpec as P

B = 512


def product(left, right):
    return jnp.dot(left, right, precision=lax.Precision.HIGHEST, preferred_element_type=jnp.float32)


def newton_inverse(matrix):
    identity = jnp.eye(matrix.shape[0], dtype=jnp.float32)
    initial = 2.0 * identity - matrix
    return product(initial, 2.0 * identity - product(matrix, initial))


def local(pivot, col_panel, row_panel, trailing):
    gathered_cols = lax.all_gather(col_panel, "col", axis=1, tiled=True)
    gathered_rows = lax.all_gather(row_panel, "row", axis=0, tiled=True)
    top_left = pivot[:B, :B]
    top_right = pivot[:B, B:]
    low_left = pivot[B:, :B]
    low_right = pivot[B:, B:]
    inverse_one = newton_inverse(top_left)
    multiplier = product(low_left, inverse_one)
    schur = low_right - product(multiplier, top_right)
    inverse_two = newton_inverse(schur)
    factor_one = product(gathered_cols[:, :B], inverse_one)
    factor_two = product(gathered_cols[:, B:] - product(factor_one, top_right), inverse_two)
    first_rows = gathered_rows[:B]
    rows_two = gathered_rows[B:] - product(multiplier, first_rows)
    return trailing - product(factor_one, first_rows) - product(factor_two, rows_two)


def solution(mesh):
    return jax.shard_map(
        local,
        mesh=mesh,
        in_specs=(P(), P("row", "col"), P("row", "col"), P("row", "col")),
        out_specs=P("row", "col"),
        check_vma=False,
    )
```

profile of v0, /device:TPU:9, one launch (start us, length us, event | category | flops | bytes accessed | tf_op | source)
XLA Modules:
  0.0 91.9 jit_solution(5261622955538227202)
XLA Ops:
  6.5 0.0 all-gather.5.cloned.1.call-start
  6.5 0.7 all-gather.5.cloned.1.call-update
  7.3 0.0 all-gather.3.cloned.1.call-start
  7.3 0.7 all-gather.3.cloned.1.call-update
  8.0 0.0 copy-start
  8.0 3.7 %select_subtract_fusion.2 = f32[512,512]{1,0:T(8,128)S(1)} fusion(f32[1024,1024]{1,0:T(8,128)} %param.4), kind=kOutput, calls=%fused_computation.2 | convolution fusion | flops 1612185600 | bytes 3145728 | tf_op jit(solution)/shard_map/dot_general | solution.py:10
  11.7 3.1 %fusion = f32[512,512]{1,0:T(8,128)S(1)} fusion(f32[512,512]{1,0:T(8,128)S(1)} %select_subtract_fusion.2, f32[1024,1024]{1,0:T(8,128)} %param.4), kind=kOutput, calls=%fused_computation.7 | convolution fusion | flops 1611399168 | bytes 3145728 | tf_op jit(solution)/shard_map/dot_general | solution.py:10
  14.9 0.0 copy-done
  14.9 3.5 %fusion.4 = f32[512,512]{1,0:T(8,128)S(1)} fusion(f32[512,512]{1,0:T(8,128)S(1)} %fusion, f32[1024,1024]{1,0:T(8,128)S(1)} %copy-done), kind=kOutput, calls=%fused_computation.14 | convolution fusion | flops 1610612736 | bytes 3145728 | tf_op jit(solution)/shard_map/dot_general | solution.py:10
  18.3 1.8 %convolution_subtract_fusion = f32[512,512]{1,0:T(8,128)S(1)} fusion(f32[512,512]{1,0:T(8,128)S(1)} %fusion.4, f32[1024,1024]{1,0:T(8,128)S(1)} %copy-done), kind=kOutput, calls=%fused_computation.4 | convolution fusion | flops 1610874880 | bytes 4194304 | tf_op jit(solution)/shard_map/dot_general | solution.py:10
  20.2 1.9 %select_subtract_fusion = f32[512,512]{1,0:T(8,128)S(1)} fusion(f32[512,512]{1,0:T(8,128)S(1)} %convolution_subtract_fusion), kind=kOutput, calls=%fused_computation | convolution fusion | flops 1612185600 | bytes 2097152 | tf_op jit(solution)/shard_map/dot_general | solution.py:10
  22.1 2.1 %fusion.1 = f32[512,512]{1,0:T(8,128)S(1)} fusion(f32[512,512]{1,0:T(8,128)S(1)} %select_subtract_fusion, f32[512,512]{1,0:T(8,128)S(1)} %convolution_subtract_fusion), kind=kOutput, calls=%fused_computation.8 | convolution fusion | flops 1611399168 | bytes 3145728 | tf_op jit(solution)/shard_map/dot_general | solution.py:10
  24.2 12.5 %all-gather.5.cloned.1.call-done = f32[1024,256]{1,0:T(8,128)} async-done(((f32[256,256]{1,0:T(8,128)}), f32[1024,256]{1,0:T(8,128)}) %all-gather.5.cloned.1.call-update) | async-done | bytes 1048592 | tf_op jit(solution)/shard_map/all_gather | solution.py:21
  36.7 3.8 %convolution_subtract_fusion.3 = f32[512,256]{1,0:T(8,128)} fusion(f32[512,512]{1,0:T(8,128)S(1)} %fusion.4, f32[1024,256]{1,0:T(8,128)} %all-gather.5.cloned.1.call-done), kind=kOutput, calls=%fused_computation.10 | convolution fusion | flops 805437440 | bytes 2621440 | tf_op jit(solution)/shard_map/dot_general | solution.py:10
  40.5 30.8 %all-gather.3.cloned.1.call-done = f32[512,1024]{1,0:T(8,128)} async-done(((f32[512,128]{1,0:T(8,128)}), f32[512,1024]{1,0:T(8,128)}) %all-gather.3.cloned.1.call-update) | async-done | bytes 2097168 | tf_op jit(solution)/shard_map/all_gather | solution.py:20
  71.3 4.7 %fusion.2 = f32[512,512]{1,0:T(8,128)S(1)} fusion(f32[512,512]{1,0:T(8,128)S(1)} %fusion, f32[512,1024]{1,0:T(8,128)} %all-gather.3.cloned.1.call-done), kind=kOutput, calls=%fused_computation.12 | convolution fusion | flops 1610612736 | bytes 3145728 | tf_op jit(solution)/shard_map/dot_general | solution.py:10
  76.0 0.0 copy-start.2
  76.0 0.0 copy-start.3
  76.0 0.0 copy-start.1
  76.0 3.5 %convolution_subtract_fusion.1 = f32[512,512]{1,0:T(8,128)S(1)} fusion(f32[512,512]{1,0:T(8,128)S(1)} %fusion.2, f32[512,1024]{1,0:T(8,128)} %all-gather.3.cloned.1.call-done, f32[1024,1024]{1,0:T(8,128)} %param.4), kind=kOutput, calls=%fused_computation.5 | convolution fusion | flops 1610874880 | bytes 4194304 | tf_op jit(solution)/shard_map/dot_general | solution.py:10
  79.5 1.8 %fusion.28 = f32[512,512]{1,0:T(8,128)S(1)} fusion(f32[512,512]{1,0:T(8,128)S(1)} %convolution_subtract_fusion.1, f32[512,512]{1,0:T(8,128)S(1)} %fusion.1), kind=kOutput, calls=%fused_computation.39 | convolution fusion | flops 1610612736 | bytes 3145728 | tf_op jit(solution)/shard_map/dot_general | solution.py:10
  81.4 0.0 copy-done.2
  81.4 0.0 copy-done.3
  81.4 1.8 %convolution_subtract_fusion.4 = f32[512,256]{1,0:T(8,128)S(1)} fusion(f32[512,256]{1,0:T(8,128)S(1)} %copy-done.3, f32[512,512]{1,0:T(8,128)S(1)} %fusion.2, f32[1024,256]{1,0:T(8,128)S(1)} %copy-done.2), kind=kOutput, calls=%fused_computation.11 | convolution fusion | flops 805437440 | bytes 2621440 | tf_op jit(solution)/shard_map/dot_general | solution.py:10
  83.2 0.0 copy-done.1
  83.2 1.8 %convolution_subtract_fusion.2 = f32[512,256]{1,0:T(8,128)} fusion(f32[512,256]{1,0:T(8,128)S(1)} %convolution_subtract_fusion.4, f32[512,512]{1,0:T(8,128)S(1)} %fusion.28, f32[512,256]{1,0:T(8,128)S(1)} %copy-done.1), kind=kOutput, calls=%fused_computation.9 | convolution fusion | flops 805437440 | bytes 2621440 | tf_op jit(solution)/shard_map/dot_general | solution.py:10
Async XLA Ops:
  6.5 30.2 %all-gather.5.cloned.1.call-start = ((), (), s32[]{:S(2)}) async-start(), calls=%async_computation.1 | async-start | bytes 1310720 | tf_op jit(solution)/shard_map/all_gather | solution.py:21
  7.3 64.0 %all-gather.3.cloned.1.call-start = ((), (), s32[]{:S(2)}) async-start(), calls=%async_computation | async-start | bytes 2359296 | tf_op jit(solution)/shard_map/all_gather | solution.py:20
  8.0 6.9 %copy-start = (f32[1024,1024]{1,0:T(8,128)S(1)}, f32[1024,1024]{1,0:T(8,128)}, u32[]{:S(2)}) copy-start(f32[1024,1024]{1,0:T(8,128)} %param.4) | copy-start | bytes 12582916
  76.0 5.4 %copy-start.2 = (f32[1024,256]{1,0:T(8,128)S(1)}, f32[1024,256]{1,0:T(8,128)}, u32[]{:S(2)}) copy-start(f32[1024,256]{1,0:T(8,128)} %all-gather.5.cloned.1.call-done) | copy-start | bytes 3145732
  76.0 5.4 %copy-start.3 = (f32[512,256]{1,0:T(8,128)S(1)}, f32[512,256]{1,0:T(8,128)}, u32[]{:S(2)}) copy-start(f32[512,256]{1,0:T(8,128)} %param.7) | copy-start | bytes 1572868
  76.0 7.3 %copy-start.1 = (f32[512,256]{1,0:T(8,128)S(1)}, f32[512,256]{1,0:T(8,128)}, u32[]{:S(2)}) copy-start(f32[512,256]{1,0:T(8,128)} %convolution_subtract_fusion.3) | copy-start | bytes 1572868
Sparse Core Ops, SparseCore 0:
  9.2 27.4 all-gather.4
  38.3 32.9 all-gather.2
where the time goes:
time: 92.1 us; the launch traced here: 91.9 us
  waiting for transfers between devices  44.7 us (49%)
  matrix products  33.6 us (36%)
  between operations  13.5 us (15%)
    dot_general x12, matrix products, product(): jnp.dot(left, right, precision=lax.Precision.HIGHEST, preferred_element_t...  33.6 us
    all_gather x1, waiting for transfers between devices, local(): gathered_cols = lax.all_gather(col_panel, 'col', axis=1, tiled=True)  30.8 us
    all_gather x1, waiting for transfers between devices, local(): gathered_rows = lax.all_gather(row_panel, 'row', axis=0, tiled=True)  12.5 us
  transfers between devices with their start and end apart: 2, of which 2 were waited for; matrix products, arithmetic and copies ran while one was open for 22% of the time, Pallas kernels for 0%

commit v1 on v0

v1 whole, which is shorter than its diff:
```python
import functools

import jax
import jax.numpy as jnp
from jax import lax
from jax.experimental import pallas as pl
from jax.experimental.pallas import tpu as pltpu
from jax.sharding import PartitionSpec as P


F32, BF16 = jnp.float32, jnp.bfloat16
HBM = pl.BlockSpec(memory_space=pltpu.HBM)
VMEM = pl.BlockSpec(memory_space=pltpu.VMEM)
CORES = 2
HOP_ONE, HOP_TWO, HOP_LAST = (1, 3, 0, 2), (2, 0, 3, 1), (3, 2, 1, 0)
SEND_ONE = ((1, 0), (3, 1), (0, 2), (2, 3))
SEND_TWO = ((2, 0), (0, 1), (3, 2), (1, 3))
SEND_ENDS, SEND_MIDDLE = ((1, 0), (2, 3)), ((1, 2), (2, 1))


def split(x):
    high = x.astype(BF16)
    return high, (x - high.astype(F32)).astype(BF16)


def dot(left, right):
    return jnp.dot(left, right, preferred_element_type=F32)


def dot3(left, right):
    (lh, ll), (rh, rl) = left, right
    return dot(lh, rh) + dot(lh, rl) + dot(ll, rh)


def eye(rows, cols, first):
    row = lax.broadcasted_iota(jnp.int32, (rows, cols), 0)
    col = lax.broadcasted_iota(jnp.int32, (rows, cols), 1)
    return jnp.where(row == col + first, 1.0, 0.0).astype(F32)


def each(n, body):
    step = min(256, n)
    for first in range(0, n, step):
        body(pl.ds(first, step), first)


def put(pair, cols, x):
    pair[0][:, cols], pair[1][:, cols] = split(x)


def product(left, right, cols):
    return dot3((left[0][...], left[1][...]), (right[0][:, cols], right[1][:, cols]))


def powers(n, x, e, f, g):
    def square(cols, _):
        s = product(e, e, cols)
        put(f, cols, s)
        x[:, cols] = x[:, cols] + s

    each(n, square)
    each(n, lambda cols, _: put(g, cols, x[:, cols] + product(e, f, cols)))


def first_kernel(pivot, g1h, g1l, vh, vl, lowh, lowl, rest, a, u, l, eh, el, fh, fl, uh, ul, sems):
    n = a.shape[0]
    g1, v, low, e, f, up = (g1h, g1l), (vh, vl), (lowh, lowl), (eh, el), (fh, fl), (uh, ul)
    copies = [
        pltpu.make_async_copy(pivot.at[pl.ds(i * n, n), pl.ds(j * n, n)], block, sems.at[2 * i + j])
        for i, j, block in ((0, 0, a), (0, 1, u), (1, 0, l), (1, 1, rest))
    ]
    for copy in copies:
        copy.start()

    def residual(cols, first):
        x = eye(n, cols.size, first) - a[:, cols]
        a[:, cols] = x
        put(e, cols, x)

    copies[0].wait()
    each(n, residual)
    powers(n, a, e, f, g1)
    copies[1].wait()
    each(n, lambda cols, _: put(up, cols, u[:, cols]))
    each(n, lambda cols, _: put(v, cols, u[:, cols] + product(g1, up, cols)))
    copies[2].wait()
    each(n, lambda cols, _: put(low, cols, l[:, cols]))
    copies[3].wait()

    def complement(cols, first):
        rest[:, cols] = eye(n, cols.size, first) - rest[:, cols]

    each(n, complement)


def first_part(pivot):
    n = pivot.shape[0] // 2
    half = jax.ShapeDtypeStruct((n, n), BF16)
    return pl.pallas_call(
        first_kernel,
        out_shape=(half,) * 6 + (jax.ShapeDtypeStruct((n, n), F32),),
        in_specs=[HBM],
        out_specs=(VMEM,) * 7,
        scratch_shapes=[pltpu.VMEM((n, n), F32)] * 3 + [pltpu.VMEM((n, n), BF16)] * 6 + [pltpu.SemaphoreType.DMA((4,))],
        cost_estimate=pl.CostEstimate(flops=18 * n * n * n, bytes_accessed=32 * n * n, transcendentals=0),
        compiler_params=pltpu.CompilerParams(vmem_limit_bytes=24 << 20),
        name="first_part",
    )(pivot)


def second_kernel(vh, vl, lowh, lowl, rest, g2h, g2l, d, eh, el, fh, fl):
    n = d.shape[0]
    v, low, g2, e, f = (vh, vl), (lowh, lowl), (g2h, g2l), (eh, el), (fh, fl)

    def residual(cols, _):
        x = rest[:, cols] + product(low, v, cols)
        d[:, cols] = x
        put(e, cols, x)

    each(n, residual)
    powers(n, d, e, f, g2)


def second_part(v, low, rest):
    n = rest.shape[0]
    half = jax.ShapeDtypeStruct((n, n), BF16)
    return pl.pallas_call(
        second_kernel,
        out_shape=(half,) * 2,
        in_specs=[VMEM] * 5,
        out_specs=(VMEM,) * 2,
        scratch_shapes=[pltpu.VMEM((n, n), F32)] + [pltpu.VMEM((n, n), BF16)] * 4,
        cost_estimate=pl.CostEstimate(flops=18 * n * n * n, bytes_accessed=16 * n * n, transcendentals=0),
        compiler_params=pltpu.CompilerParams(vmem_limit_bytes=24 << 20),
        name="second_part",
    )(*v, *low, rest)


def chain_kernel(g1h, g1l, vh, vl, lowh, lowl, g2h, g2l, *refs):
    rows, (yh, yl, r, rh, rl) = refs[:-5], refs[-5:]
    n = g1h.shape[0]
    deep = rows[0].shape[0]
    me = lax.axis_index("row")
    for s, piece in enumerate(rows):
        at = pl.ds(pl.multiple_of((me ^ s) * deep, deep), deep)
        x = piece[...]
        r[at, :] = x
        rh[at, :], rl[at, :] = split(x)
    upper, lower = pl.ds(0, n), pl.ds(n, n)
    full = lambda high, low: (high[...], low[...])
    ya = r[upper, :] + dot3(full(g1h, g1l), (rh[upper, :], rl[upper, :]))
    t2 = r[lower, :] - dot3(full(lowh, lowl), split(ya))
    y2 = split(t2 + dot3(full(g2h, g2l), split(t2)))
    yh[lower, :], yl[lower, :] = y2
    yh[upper, :], yl[upper, :] = split(ya - dot3(full(vh, vl), y2))


def chain_part(g1, v, low, g2, rows):
    n = g1[0].shape[0]
    width = rows[0].shape[1]
    half = jax.ShapeDtypeStruct((2 * n, width), BF16)
    return pl.pallas_call(
        chain_kernel,
        out_shape=(half,) * 2,
        in_specs=[VMEM] * (8 + len(rows)),
        out_specs=(VMEM,) * 2,
        scratch_shapes=[pltpu.VMEM((2 * n, width), F32)] + [pltpu.VMEM((2 * n, width), BF16)] * 2,
        cost_estimate=pl.CostEstimate(flops=24 * n * n * width, bytes_accessed=16 * n * (n + width), transcendentals=0),
        compiler_params=pltpu.CompilerParams(vmem_limit_bytes=16 << 20),
        name="chain_part",
    )(*g1, *v, *low, *g2, *rows)


def position():
    me = lax.axis_index("col")
    return me // CORES, me % CORES


def entry(table, index):
    value = jnp.int32(table[0])
    for i, x in enumerate(table[1:], 1):
        value = jnp.where(index == i, x, value)
    return value


def times(table, own, other, yh, yl):
    chip, core = position()
    tall = CORES * own.shape[1]
    at = pl.ds(pl.multiple_of(entry(table, chip) * tall, tall), tall)
    both = jnp.concatenate([jnp.where(core == 0, own, other), jnp.where(core == 0, other, own)], axis=1)
    return dot3(split(both), (yh[at, :], yl[at, :]))


def update_kernel(tables, trail, yh, yl, *refs):
    pieces, out = refs[:-1], refs[-1]
    total = trail[...]
    for i, table in enumerate(tables):
        total = total - times(table, pieces[2 * i][...], pieces[2 * i + 1][...], yh, yl)
    out[...] = total


def update_part(tables, trail, y, pieces):
    m, width = trail.shape
    wide = pieces[0].shape[1]
    return pl.pallas_call(
        functools.partial(update_kernel, tables),
        out_shape=jax.ShapeDtypeStruct((m, width), F32),
        in_specs=[VMEM] * (3 + len(pieces)),
        out_specs=VMEM,
        cost_estimate=pl.CostEstimate(
            flops=6 * m * width * wide * len(pieces), bytes_accessed=4 * m * (2 * width + wide * len(pieces)), transcendentals=0
        ),
        compiler_params=pltpu.CompilerParams(vmem_limit_bytes=16 << 20),
        name="update_part",
    )(trail, *y, *pieces)


def last_kernel(part, yh, yl, end, middle, end_other, middle_other, out):
    chip, _ = position()
    inner = (chip != 0) & (chip != len(HOP_LAST) - 1)
    own = jnp.where(inner, middle[...], end[...])
    other = jnp.where(inner, middle_other[...], end_other[...])
    out[...] = part[...] - times(HOP_LAST, own, other, yh, yl)


def last_part(part, y, *pieces):
    m, width = part.shape
    wide = pieces[0].shape[1]
    return pl.pallas_call(
        last_kernel,
        out_shape=jax.ShapeDtypeStruct((m, width), F32),
        in_specs=[VMEM] * 7,
        out_specs=VMEM,
        cost_estimate=pl.CostEstimate(flops=12 * m * width * wide, bytes_accessed=4 * m * (2 * width + 4 * wide), transcendentals=0),
        compiler_params=pltpu.CompilerParams(vmem_limit_bytes=8 << 20),
        name="last_part",
    )(part, *y, *pieces)


def local(n_row, pivot, col_panel, row_panel, trailing):
    def send(x, pairs):
        return lax.ppermute(x, "col", [(CORES * a + c, CORES * b + c) for a, b in pairs for c in range(CORES)])

    def exchange(x, chips):
        return lax.ppermute(x, "col", [(CORES * a + c, CORES * a + (c ^ 1)) for a in chips for c in range(CORES)])

    def row(s):
        return lax.ppermute(row_panel, "row", [(i, i ^ s) for i in range(n_row)])

    chips = tuple(range(len(HOP_ONE)))
    ends, inner = (chips[0], chips[-1]), chips[1:-1]
    one = send(col_panel, SEND_ONE)
    two = send(col_panel, SEND_TWO)
    end = send(one, SEND_ENDS)
    middle = send(col_panel, SEND_MIDDLE)
    rows = [row_panel] + [row(s) for s in range(1, n_row)]
    *pairs, rest = first_part(pivot)
    g1, v, low = pairs[0:2], pairs[2:4], pairs[4:6]
    g2 = second_part(v, low, rest)
    y = chain_part(g1, v, low, g2, rows)
    pieces = [x for mine in (col_panel, one, two) for x in (mine, exchange(mine, chips))]
    part = update_part((chips, HOP_ONE, HOP_TWO), trailing, y, pieces)
    end_other, middle_other = exchange(end, ends), exchange(middle, inner)
    return last_part(part, y, end, middle, end_other, middle_other)


def exact(left, right):
    return jnp.dot(left, right, precision=lax.Precision.HIGHEST, preferred_element_type=F32)


def newton_inverse(matrix):
    identity = jnp.eye(matrix.shape[0], dtype=F32)
    initial = 2.0 * identity - matrix
    return exact(initial, 2.0 * identity - exact(matrix, initial))


def gathered(pivot, col_panel, row_panel, trailing):
    cols = lax.all_gather(col_panel, "col", axis=1, tiled=True)
    rows = lax.all_gather(row_panel, "row", axis=0, tiled=True)
    n = pivot.shape[0] // 2
    top_left, top_right, low_left, low_right = pivot[:n, :n], pivot[:n, n:], pivot[n:, :n], pivot[n:, n:]
    inverse_one = newton_inverse(top_left)
    multiplier = exact(low_left, inverse_one)
    inverse_two = newton_inverse(low_right - exact(multiplier, top_right))
    factor_one = exact(cols[:, :n], inverse_one)
    factor_two = exact(cols[:, n:] - exact(factor_one, top_right), inverse_two)
    rows_two = rows[n:] - exact(multiplier, rows[:n])
    return trailing - exact(factor_one, rows[:n]) - exact(factor_two, rows_two)


def power_of_two(n):
    return n & (n - 1) == 0


def solution(mesh):
    n_row, n_col = mesh.shape["row"], mesh.shape["col"]
    line = n_col == CORES * len(HOP_ONE) and power_of_two(n_row)

    def body(pivot, col_panel, row_panel, trailing):
        if line:
            return local(n_row, pivot, col_panel, row_panel, trailing)
        return gathered(pivot, col_panel, row_panel, trailing)

    return jax.shard_map(
        body,
        mesh=mesh,
        in_specs=(P(), P("row", "col"), P("row", "col"), P("row", "col")),
        out_specs=P("row", "col"),
        check_vma=False,
    )
```

time: 92.1 us -> 35 us (0.38)
  the two profiles are of different devices: /device:TPU:9 before, /device:TPU:1 now
where the time goes in v1:
time: 35 us; the launch traced here: 34.8 us
  starting transfers between devices  14.8 us (42%)
  Pallas kernels  12.7 us (36%)
  waiting for transfers between devices  4.86 us (14%)
  local copies, waits for them, and re-layouts  2.2 us (6%)
    ppermute x5, starting transfers between devices, exchange(): lax.ppermute(x, 'col', [(CORES * a + c, CORES * a + (c ^ 1)) for a in chi...  7.11 us
    ppermute x4, starting transfers between devices, send(): lax.ppermute(x, 'col', [(CORES * a + c, CORES * b + c) for a, b in pairs...  4.26 us
    pallas_call x1, Pallas kernels, first_part(): pl.pallas_call(first_kernel, out_shape=(half,) * 6 + (jax.ShapeDtypeStruc...  4.08 us
    pallas_call x1, Pallas kernels, chain_part(): pl.pallas_call(chain_kernel, out_shape=(half,) * 2, in_specs=[VMEM] * (8...  3.81 us
    ppermute x3, starting transfers between devices, row(): return lax.ppermute(row_panel, 'row', [(i, i ^ s) for i in range(n_row)])  3.47 us
    pallas_call x1, Pallas kernels, second_part(): pl.pallas_call(second_kernel, out_shape=(half,) * 2, in_specs=[VMEM] * 5,...  2.85 us
    ppermute x3, waiting for transfers between devices, row(): return lax.ppermute(row_panel, 'row', [(i, i ^ s) for i in range(n_row)])  2.47 us
    ppermute x4, waiting for transfers between devices, send(): lax.ppermute(x, 'col', [(CORES * a + c, CORES * b + c) for a, b in pairs...  2.37 us
  transfers between devices with their start and end apart: 12, of which 3 were waited for; matrix products, arithmetic and copies ran while one was open for 0% of the time, Pallas kernels for 33%

profile of v1, /device:TPU:1, one launch (start us, length us, event | category | flops | bytes accessed | tf_op | source)
XLA Modules:
  0.0 34.8 jit_solution(14520687916025631190)
XLA Ops:
  0.0 0.0 copy-start.1
  0.0 2.0 %collective-permute-start = (f32[256,256]{1,0:T(8,128)}, f32[256,256]{1,0:T(8,128)S(1)}, u32[]{:S(2)}, u32[]{:S(2)}) collective-permute-start(f32[256,256]{1,0:T(8,128)} %refs_0_.2), channel_id=1, source_target_pairs={{0,8},{8,0},{16,24},{24,16},{1,9},{9,1},{17,25},{25,17},{2,10},{10... | collective-permute-start | bytes 786440 | tf_op jit(solution)/shard_map/ppermute | solution.py:248
  2.0 2.3 %collective-permute-start.4 = (f32[512,128]{1,0:T(8,128)}, f32[512,128]{1,0:T(8,128)S(1)}, u32[]{:S(2)}, u32[]{:S(2)}) collective-permute-start(f32[512,128]{1,0:T(8,128)} %refs_0_.3), channel_id=1, source_target_pairs={{2,0},{3,1},{6,2},{7,3},{0,4},{1,5},{4,6},{5,7},{10,8},{11,9},{14,... | collective-permute-start | bytes 786440 | tf_op jit(solution)/shard_map/ppermute | solution.py:242
  4.3 1.2 %collective-permute-start.1 = (f32[256,256]{1,0:T(8,128)}, f32[256,256]{1,0:T(8,128)S(1)}, u32[]{:S(2)}, u32[]{:S(2)}) collective-permute-start(f32[256,256]{1,0:T(8,128)} %refs_0_.2), channel_id=1, source_target_pairs={{0,16},{8,24},{16,0},{24,8},{1,17},{9,25},{17,1},{25,9},{2,18},{10... | collective-permute-start | bytes 786440 | tf_op jit(solution)/shard_map/ppermute | solution.py:248
  5.6 0.2 collective-permute-start.2
  5.8 0.0 collective-permute-start.6
  5.8 2.5 %collective-permute-done.refs_1_ = f32[256,256]{1,0:T(8,128)S(1)} collective-permute-done((f32[256,256]{1,0:T(8,128)}, f32[256,256]{1,0:T(8,128)S(1)}, u32[]{:S(2)}, u32[]{:S(2)}) %collective-permute-start) | collective-permute-done | bytes 262176 | tf_op jit(solution)/shard_map/ppermute | solution.py:248
  8.2 0.7 %collective-permute-start.9 = (f32[512,128]{1,0:T(8,128)}, f32[512,128]{1,0:T(8,128)S(1)}, u32[]{:S(2)}, u32[]{:S(2)}) collective-permute-start(f32[512,128]{1,0:T(8,128)} %refs_0_.3), channel_id=1, source_target_pairs={{2,4},{3,5},{4,2},{5,3},{10,12},{11,13},{12,10},{13,11},{18,20},{1... | collective-permute-start | bytes 786440 | tf_op jit(solution)/shard_map/ppermute | solution.py:242
  8.9 0.5 %collective-permute-done.4.refs_2_ = f32[512,128]{1,0:T(8,128)S(1)} collective-permute-done((f32[512,128]{1,0:T(8,128)}, f32[512,128]{1,0:T(8,128)S(1)}, u32[]{:S(2)}, u32[]{:S(2)}) %collective-permute-start.4) | collective-permute-done | bytes 262176 | tf_op jit(solution)/shard_map/ppermute | solution.py:242
  9.4 1.3 %collective-permute-start.8 = (f32[512,128]{1,0:T(8,128)S(1)}, f32[512,128]{1,0:T(8,128)S(1)}, u32[]{:S(2)}, u32[]{:S(2)}) collective-permute-start(f32[512,128]{1,0:T(8,128)S(1)} %collective-permute-done.4.refs_2_), channel_id=1, source_target_pairs={{2,0},{3,1},{4,6},{5,7},{10,8},{11,9},{12,14},{13,15},{18,16},{19,... | collective-permute-start | bytes 786440 | tf_op jit(solution)/shard_map/ppermute | solution.py:242
  10.7 0.0 copy-start.2
  10.7 2.2 %copy-done.2 = f32[1024,1024]{1,0:T(8,128)S(1)} copy-done((f32[1024,1024]{1,0:T(8,128)S(1)}, f32[1024,1024]{1,0:T(8,128)}, u32[]{:S(2)}) %copy-start.2) | copy-done | bytes 4194328
  12.9 4.1 %first_part.1 = (bf16[512,512]{1,0:T(8,128)(2,1)S(1)}, bf16[512,512]{1,0:T(8,128)(2,1)S(1)}, bf16[512,512]{1,0:T(8,128)(2,1)S(1)}, bf16[512,512]{1,0:T(8,128)(2,...) custom-call(f32[1024,1024]{1,0:T(8,128)S(1)} %copy-done.2), custom_call_target="tpu_custom_call" | custom-call | flops 2415919104 | bytes 8388608 | tf_op jit(solution)/shard_map/first_part/pallas_call | solution.py:99
  17.0 0.0 collective-permute-done.1.refs_2_
  17.0 0.0 copy-done.1
  17.0 3.3 %collective-permute-start.3 = (f32[512,128]{1,0:T(8,128)S(1)}, f32[512,128]{1,0:T(8,128)S(1)}, u32[]{:S(2)}, u32[]{:S(2)}) collective-permute-start(f32[512,128]{1,0:T(8,128)S(1)} %copy-done.1), channel_id=1, source_target_pairs={{0,1},{1,0},{2,3},{3,2},{4,5},{5,4},{6,7},{7,6},{8,9},{9,8},{10,11... | collective-permute-start | bytes 786440 | tf_op jit(solution)/shard_map/ppermute | solution.py:245
  20.3 0.0 collective-permute-done.2.refs_3_
  20.3 0.1 collective-permute-start.5
  20.4 0.0 collective-permute-done.6.refs_4_
  20.4 0.4 %collective-permute-start.7 = (f32[512,128]{1,0:T(8,128)S(1)}, f32[512,128]{1,0:T(8,128)S(1)}, u32[]{:S(2)}, u32[]{:S(2)}) collective-permute-start(f32[512,128]{1,0:T(8,128)S(1)} %collective-permute-done.6.refs_4_), channel_id=1, source_target_pairs={{0,1},{1,0},{2,3},{3,2},{4,5},{5,4},{6,7},{7,6},{8,9},{9,8},{10,11... | collective-permute-start | bytes 786440 | tf_op jit(solution)/shard_map/ppermute | solution.py:245
  20.8 0.0 collective-permute-done.9.middle
  20.8 0.7 %collective-permute-start.11 = (f32[512,128]{1,0:T(8,128)S(1)}, f32[512,128]{1,0:T(8,128)S(1)}, u32[]{:S(2)}, u32[]{:S(2)}) collective-permute-start(f32[512,128]{1,0:T(8,128)S(1)} %collective-permute-done.9.middle), channel_id=1, source_target_pairs={{2,3},{3,2},{4,5},{5,4},{10,11},{11,10},{12,13},{13,12},{18,19},{1... | collective-permute-start | bytes 786440 | tf_op jit(solution)/shard_map/ppermute | solution.py:245
  21.5 1.9 %collective-permute-done.8.end = f32[512,128]{1,0:T(8,128)S(1)} collective-permute-done((f32[512,128]{1,0:T(8,128)S(1)}, f32[512,128]{1,0:T(8,128)S(1)}, u32[]{:S(2)}, u32[]{:S(2)}) %collective-permute-start.8) | collective-permute-done | bytes 262176 | tf_op jit(solution)/shard_map/ppermute | solution.py:242
  23.4 2.6 %collective-permute-start.10 = (f32[512,128]{1,0:T(8,128)S(1)}, f32[512,128]{1,0:T(8,128)S(1)}, u32[]{:S(2)}, u32[]{:S(2)}) collective-permute-start(f32[512,128]{1,0:T(8,128)S(1)} %collective-permute-done.8.end), channel_id=1, source_target_pairs={{0,1},{1,0},{6,7},{7,6},{8,9},{9,8},{14,15},{15,14},{16,17},{17,16... | collective-permute-start | bytes 786440 | tf_op jit(solution)/shard_map/ppermute | solution.py:245
  26.0 0.0 copy-start.3
  26.0 2.9 %second_part.1 = (bf16[512,512]{1,0:T(8,128)(2,1)S(1)}, bf16[512,512]{1,0:T(8,128)(2,1)S(1)}) custom-call(bf16[512,512]{1,0:T(8,128)(2,1)S(1)} %get-tuple-element.18.vh, bf16[512,512]{1,0:T(8,128)(2,1)S(1)} %get-tuple-element.19.vl, bf16[512,512]{1,0:T(8,128)(2,1)S(1)} %get-tuple-element.20.lowh, bf16[512,512]{1,0:T(8,128)(2,1)S(1)} %get-tuple-element.21.lowl, ...), custom_call_target="tpu_custom_call" | custom-call | flops 2415919104 | bytes 4194304 | tf_op jit(solution)/shard_map/second_part/pallas_call | solution.py:127
  28.9 0.0 copy-start
  28.9 0.0 copy-done.3
  28.9 3.8 %chain_part.1 = (bf16[1024,256]{1,0:T(8,128)(2,1)S(1)}, bf16[1024,256]{1,0:T(8,128)(2,1)S(1)}) custom-call(bf16[512,512]{1,0:T(8,128)(2,1)S(1)} %get-tuple-element.16.g1h, bf16[512,512]{1,0:T(8,128)(2,1)S(1)} %get-tuple-element.17.g1l, bf16[512,512]{1,0:T(8,128)(2,1)S(1)} %get-tuple-element.18.vh, bf16[512,512]{1,0:T(8,128)(2,1)S(1)} %get-tuple-element.19.vl, ...), custom_call_target="tpu_custom_call" | custom-call | flops 1610612736 | bytes 6291456 | tf_op jit(solution)/shard_map/chain_part/pallas_call | solution.py:162
  32.7 0.0 collective-permute-done.3.refs_1_
  32.7 0.0 collective-permute-done.5.refs_3_
  32.7 0.0 collective-permute-done.7.refs_5_
  32.8 0.0 copy-done
  32.8 0.8 %update_part.1.part = f32[512,256]{1,0:T(8,128)S(1)} custom-call(f32[512,256]{1,0:T(8,128)S(1)} %copy-done, bf16[1024,256]{1,0:T(8,128)(2,1)S(1)} %get-tuple-element.25.yh, bf16[1024,256]{1,0:T(8,128)(2,1)S(1)} %get-tuple-element.26.yl, f32[512,128]{1,0:T(8,128)S(1)} %copy-done.1, f32[512,128]{1,0:T(8,128)S(1)} %collective-permute-done.3.refs_1_, ...), custom_call_target="tpu_custom_call" | custom-call | flops 603979776 | bytes 2621440 | tf_op jit(solution)/shard_map/update_part/pallas_call | solution.py:205
  33.6 0.0 collective-permute-done.11.middle_other
  33.6 0.0 collective-permute-done.10.end_other
  33.6 1.2 %last_part.1 = f32[512,256]{1,0:T(8,128)} custom-call(f32[512,256]{1,0:T(8,128)S(1)} %update_part.1.part, bf16[1024,256]{1,0:T(8,128)(2,1)S(1)} %get-tuple-element.25.yh, bf16[1024,256]{1,0:T(8,128)(2,1)S(1)} %get-tuple-element.26.yl, f32[512,128]{1,0:T(8,128)S(1)} %collective-permute-done.8.end, f32[512,128]{1,0:T(8,128)S(1)} %collective-permute-done.9.middle, ...), custom_call_target="tpu_custom_call" | custom-call | flops 201326592 | bytes 2097152 | tf_op jit(solution)/shard_map/last_part/pallas_call | solution.py:229
Async XLA Ops:
  0.0 17.0 %copy-start.1 = (f32[512,128]{1,0:T(8,128)S(1)}, f32[512,128]{1,0:T(8,128)}, u32[]{:S(2)}) copy-start(f32[512,128]{1,0:T(8,128)} %refs_0_.3) | copy-start | bytes 786436
  0.0 8.2 %collective-permute-start = (f32[256,256]{1,0:T(8,128)}, f32[256,256]{1,0:T(8,128)S(1)}, u32[]{:S(2)}, u32[]{:S(2)}) collective-permute-start(f32[256,256]{1,0:T(8,128)} %refs_0_.2), channel_id=1, source_target_pairs={{0,8},{8,0},{16,24},{24,16},{1,9},{9,1},{17,25},{25,17},{2,10},{10... | collective-permute-start | bytes 786440 | tf_op jit(solution)/shard_map/ppermute | solution.py:248
  2.0 7.4 %collective-permute-start.4 = (f32[512,128]{1,0:T(8,128)}, f32[512,128]{1,0:T(8,128)S(1)}, u32[]{:S(2)}, u32[]{:S(2)}) collective-permute-start(f32[512,128]{1,0:T(8,128)} %refs_0_.3), channel_id=1, source_target_pairs={{2,0},{3,1},{6,2},{7,3},{0,4},{1,5},{4,6},{5,7},{10,8},{11,9},{14,... | collective-permute-start | bytes 786440 | tf_op jit(solution)/shard_map/ppermute | solution.py:242
  4.3 12.6 %collective-permute-start.1 = (f32[256,256]{1,0:T(8,128)}, f32[256,256]{1,0:T(8,128)S(1)}, u32[]{:S(2)}, u32[]{:S(2)}) collective-permute-start(f32[256,256]{1,0:T(8,128)} %refs_0_.2), channel_id=1, source_target_pairs={{0,16},{8,24},{16,0},{24,8},{1,17},{9,25},{17,1},{25,9},{2,18},{10... | collective-permute-start | bytes 786440 | tf_op jit(solution)/shard_map/ppermute | solution.py:248
  5.6 14.7 %collective-permute-start.2 = (f32[256,256]{1,0:T(8,128)}, f32[256,256]{1,0:T(8,128)S(1)}, u32[]{:S(2)}, u32[]{:S(2)}) collective-permute-start(f32[256,256]{1,0:T(8,128)} %refs_0_.2), channel_id=1, source_target_pairs={{0,24},{8,16},{16,8},{24,0},{1,25},{9,17},{17,9},{25,1},{2,26},{10... | collective-permute-start | bytes 786440 | tf_op jit(solution)/shard_map/ppermute | solution.py:248
  5.8 14.6 %collective-permute-start.6 = (f32[512,128]{1,0:T(8,128)}, f32[512,128]{1,0:T(8,128)S(1)}, u32[]{:S(2)}, u32[]{:S(2)}) collective-permute-start(f32[512,128]{1,0:T(8,128)} %refs_0_.3), channel_id=1, source_target_pairs={{4,0},{5,1},{0,2},{1,3},{6,4},{7,5},{2,6},{3,7},{12,8},{13,9},{8,1... | collective-permute-start | bytes 786440 | tf_op jit(solution)/shard_map/ppermute | solution.py:242
  8.2 12.6 %collective-permute-start.9 = (f32[512,128]{1,0:T(8,128)}, f32[512,128]{1,0:T(8,128)S(1)}, u32[]{:S(2)}, u32[]{:S(2)}) collective-permute-start(f32[512,128]{1,0:T(8,128)} %refs_0_.3), channel_id=1, source_target_pairs={{2,4},{3,5},{4,2},{5,3},{10,12},{11,13},{12,10},{13,11},{18,20},{1... | collective-permute-start | bytes 786440 | tf_op jit(solution)/shard_map/ppermute | solution.py:242
  9.4 13.9 %collective-permute-start.8 = (f32[512,128]{1,0:T(8,128)S(1)}, f32[512,128]{1,0:T(8,128)S(1)}, u32[]{:S(2)}, u32[]{:S(2)}) collective-permute-start(f32[512,128]{1,0:T(8,128)S(1)} %collective-permute-done.4.refs_2_), channel_id=1, source_target_pairs={{2,0},{3,1},{4,6},{5,7},{10,8},{11,9},{12,14},{13,15},{18,16},{19,... | collective-permute-start | bytes 786440 | tf_op jit(solution)/shard_map/ppermute | solution.py:242
  10.7 2.2 %copy-start.2 = (f32[1024,1024]{1,0:T(8,128)S(1)}, f32[1024,1024]{1,0:T(8,128)}, u32[]{:S(2)}) copy-start(f32[1024,1024]{1,0:T(8,128)} %pivot.1) | copy-start | bytes 12582916
  17.0 15.7 %collective-permute-start.3 = (f32[512,128]{1,0:T(8,128)S(1)}, f32[512,128]{1,0:T(8,128)S(1)}, u32[]{:S(2)}, u32[]{:S(2)}) collective-permute-start(f32[512,128]{1,0:T(8,128)S(1)} %copy-done.1), channel_id=1, source_target_pairs={{0,1},{1,0},{2,3},{3,2},{4,5},{5,4},{6,7},{7,6},{8,9},{9,8},{10,11... | collective-permute-start | bytes 786440 | tf_op jit(solution)/shard_map/ppermute | solution.py:245
  20.3 12.5 %collective-permute-start.5 = (f32[512,128]{1,0:T(8,128)S(1)}, f32[512,128]{1,0:T(8,128)S(1)}, u32[]{:S(2)}, u32[]{:S(2)}) collective-permute-start(f32[512,128]{1,0:T(8,128)S(1)} %collective-permute-done.4.refs_2_), channel_id=1, source_target_pairs={{0,1},{1,0},{2,3},{3,2},{4,5},{5,4},{6,7},{7,6},{8,9},{9,8},{10,11... | collective-permute-start | bytes 786440 | tf_op jit(solution)/shard_map/ppermute | solution.py:245
  20.4 12.4 %collective-permute-start.7 = (f32[512,128]{1,0:T(8,128)S(1)}, f32[512,128]{1,0:T(8,128)S(1)}, u32[]{:S(2)}, u32[]{:S(2)}) collective-permute-start(f32[512,128]{1,0:T(8,128)S(1)} %collective-permute-done.6.refs_4_), channel_id=1, source_target_pairs={{0,1},{1,0},{2,3},{3,2},{4,5},{5,4},{6,7},{7,6},{8,9},{9,8},{10,11... | collective-permute-start | bytes 786440 | tf_op jit(solution)/shard_map/ppermute | solution.py:245
  20.8 12.8 %collective-permute-start.11 = (f32[512,128]{1,0:T(8,128)S(1)}, f32[512,128]{1,0:T(8,128)S(1)}, u32[]{:S(2)}, u32[]{:S(2)}) collective-permute-start(f32[512,128]{1,0:T(8,128)S(1)} %collective-permute-done.9.middle), channel_id=1, source_target_pairs={{2,3},{3,2},{4,5},{5,4},{10,11},{11,10},{12,13},{13,12},{18,19},{1... | collective-permute-start | bytes 786440 | tf_op jit(solution)/shard_map/ppermute | solution.py:245
  23.4 10.2 %collective-permute-start.10 = (f32[512,128]{1,0:T(8,128)S(1)}, f32[512,128]{1,0:T(8,128)S(1)}, u32[]{:S(2)}, u32[]{:S(2)}) collective-permute-start(f32[512,128]{1,0:T(8,128)S(1)} %collective-permute-done.8.end), channel_id=1, source_target_pairs={{0,1},{1,0},{6,7},{7,6},{8,9},{9,8},{14,15},{15,14},{16,17},{17,16... | collective-permute-start | bytes 786440 | tf_op jit(solution)/shard_map/ppermute | solution.py:245
  26.0 2.9 %copy-start.3 = (f32[256,256]{1,0:T(8,128)S(1)}, f32[256,256]{1,0:T(8,128)}, u32[]{:S(2)}) copy-start(f32[256,256]{1,0:T(8,128)} %refs_0_.2) | copy-start | bytes 786436
  28.9 3.9 %copy-start = (f32[512,256]{1,0:T(8,128)S(1)}, f32[512,256]{1,0:T(8,128)}, u32[]{:S(2)}) copy-start(f32[512,256]{1,0:T(8,128)} %trail.1) | copy-start | bytes 1572868

commit v2 on v1

--- a/solution.py
+++ b/solution.py
@@ -9,13 +9,13 @@
 
 
 F32, BF16 = jnp.float32, jnp.bfloat16
-HBM = pl.BlockSpec(memory_space=pltpu.HBM)
 VMEM = pl.BlockSpec(memory_space=pltpu.VMEM)
 CORES = 2
 HOP_ONE, HOP_TWO, HOP_LAST = (1, 3, 0, 2), (2, 0, 3, 1), (3, 2, 1, 0)
 SEND_ONE = ((1, 0), (3, 1), (0, 2), (2, 3))
 SEND_TWO = ((2, 0), (0, 1), (3, 2), (1, 3))
-SEND_ENDS, SEND_MIDDLE = ((1, 0), (2, 3)), ((1, 2), (2, 1))
+SEND_ENDS = ((1, 0), (2, 3), (0, 1), (3, 2))
+SEND_MIDDLE = ((1, 2), (2, 1), (0, 0), (3, 3))
 
 
 def split(x):
@@ -62,78 +62,92 @@
     each(n, lambda cols, _: put(g, cols, x[:, cols] + product(e, f, cols)))
 
 
-def first_kernel(pivot, g1h, g1l, vh, vl, lowh, lowl, rest, a, u, l, eh, el, fh, fl, uh, ul, sems):
+def quadrant(n, i, j):
+    return pl.ds(i * n, n), pl.ds(j * n, n)
+
+
+def first_kernel(pivot, g1h, g1l, u, l, d, a, eh, el, fh, fl, sems):
     n = a.shape[0]
-    g1, v, low, e, f, up = (g1h, g1l), (vh, vl), (lowh, lowl), (eh, el), (fh, fl), (uh, ul)
     copies = [
-        pltpu.make_async_copy(pivot.at[pl.ds(i * n, n), pl.ds(j * n, n)], block, sems.at[2 * i + j])
-        for i, j, block in ((0, 0, a), (0, 1, u), (1, 0, l), (1, 1, rest))
+        pltpu.make_async_copy(pivot.at[quadrant(n, i, j)], block, sems.at[2 * i + j])
+        for i, j, block in ((0, 0, a), (0, 1, u), (1, 0, l), (1, 1, d))
     ]
     for copy in copies:
         copy.start()
+    copies[0].wait()
 
     def residual(cols, first):
         x = eye(n, cols.size, first) - a[:, cols]
         a[:, cols] = x
-        put(e, cols, x)
-
-    copies[0].wait()
+        put((eh, el), cols, x)
+
     each(n, residual)
-    powers(n, a, e, f, g1)
-    copies[1].wait()
+    powers(n, a, (eh, el), (fh, fl), (g1h, g1l))
+    for copy in copies[1:]:
+        copy.wait()
+
+
+def kernel_call(body, name, outs, ins, scratch, products, limit=16):
+    n = outs[0].shape[0]
+    specs = [pl.BlockSpec(memory_space=pltpu.HBM if name == "first_part" else pltpu.VMEM)] * len(ins)
+    return pl.pallas_call(
+        body,
+        out_shape=tuple(outs),
+        in_specs=specs,
+        out_specs=(VMEM,) * len(outs),
+        scratch_shapes=scratch,
+        cost_estimate=pl.CostEstimate(flops=int(6 * products * n * n * n), bytes_accessed=16 * n * n, transcendentals=0),
+        compiler_params=pltpu.CompilerParams(vmem_limit_bytes=limit << 20),
+    )(*ins)
+
+
+def half(*shape):
+    return jax.ShapeDtypeStruct(shape, BF16)
+
+
+def single(*shape):
+    return jax.ShapeDtypeStruct(shape, F32)
+
+
+def first_part(pivot):
+    n = pivot.shape[0] // 2
+    outs = [half(n, n)] * 2 + [single(n, n)] * 3
+    scratch = [pltpu.VMEM((n, n), F32)] + [pltpu.VMEM((n, n), BF16)] * 4 + [pltpu.SemaphoreType.DMA((4,))]
+    pivot = pltpu.with_memory_space_constraint(pivot, pltpu.HBM)
+    return kernel_call(first_kernel, "first_part", outs, (pivot,), scratch, 2)
+
+
+def second_kernel(g1h, g1l, u, l, d, vh, vl, lowh, lowl, e, eh, el, uh, ul):
+    n = u.shape[0]
+    g1, v, low, up = (g1h, g1l), (vh, vl), (lowh, lowl), (uh, ul)
     each(n, lambda cols, _: put(up, cols, u[:, cols]))
     each(n, lambda cols, _: put(v, cols, u[:, cols] + product(g1, up, cols)))
-    copies[2].wait()
     each(n, lambda cols, _: put(low, cols, l[:, cols]))
-    copies[3].wait()
-
-    def complement(cols, first):
-        rest[:, cols] = eye(n, cols.size, first) - rest[:, cols]
-
-    each(n, complement)
-
-
-def first_part(pivot):
-    n = pivot.shape[0] // 2
-    half = jax.ShapeDtypeStruct((n, n), BF16)
-    return pl.pallas_call(
-        first_kernel,
-        out_shape=(half,) * 6 + (jax.ShapeDtypeStruct((n, n), F32),),
-        in_specs=[HBM],
-        out_specs=(VMEM,) * 7,
-        scratch_shapes=[pltpu.VMEM((n, n), F32)] * 3 + [pltpu.VMEM((n, n), BF16)] * 6 + [pltpu.SemaphoreType.DMA((4,))],
-        cost_estimate=pl.CostEstimate(flops=18 * n * n * n, bytes_accessed=32 * n * n, transcendentals=0),
-        compiler_params=pltpu.CompilerParams(vmem_limit_bytes=24 << 20),
-        name="first_part",
-    )(pivot)
-
-
-def second_kernel(vh, vl, lowh, lowl, rest, g2h, g2l, d, eh, el, fh, fl):
-    n = d.shape[0]
-    v, low, g2, e, f = (vh, vl), (lowh, lowl), (g2h, g2l), (eh, el), (fh, fl)
-
-    def residual(cols, _):
-        x = rest[:, cols] + product(low, v, cols)
-        d[:, cols] = x
-        put(e, cols, x)
+
+    def residual(cols, first):
+        x = (eye(n, cols.size, first) - d[:, cols]) + product(low, v, cols)
+        e[:, cols] = x
+        put((eh, el), cols, x)
 
     each(n, residual)
-    powers(n, d, e, f, g2)
-
-
-def second_part(v, low, rest):
-    n = rest.shape[0]
-    half = jax.ShapeDtypeStruct((n, n), BF16)
-    return pl.pallas_call(
-        second_kernel,
-        out_shape=(half,) * 2,
-        in_specs=[VMEM] * 5,
-        out_specs=(VMEM,) * 2,
-        scratch_shapes=[pltpu.VMEM((n, n), F32)] + [pltpu.VMEM((n, n), BF16)] * 4,
-        cost_estimate=pl.CostEstimate(flops=18 * n * n * n, bytes_accessed=16 * n * n, transcendentals=0),
-        compiler_params=pltpu.CompilerParams(vmem_limit_bytes=24 << 20),
-        name="second_part",
-    )(*v, *low, rest)
+
+
+def second_part(g1, u, l, d):
+    n = u.shape[0]
+    outs = [half(n, n)] * 4 + [single(n, n)] + [half(n, n)] * 2
+    return kernel_call(second_kernel, "second_part", outs, (*g1, u, l, d), [pltpu.VMEM((n, n), BF16)] * 2, 2)
+
+
+def third_kernel(e, eh, el, g2h, g2l, x, fh, fl):
+    n = e.shape[0]
+    x[...] = e[...]
+    powers(n, x, (eh, el), (fh, fl), (g2h, g2l))
+
+
+def third_part(e, eh, el):
+    n = e.shape[0]
+    scratch = [pltpu.VMEM((n, n), F32)] + [pltpu.VMEM((n, n), BF16)] * 2
+    return kernel_call(third_kernel, "third_part", [half(n, n)] * 2, (e, eh, el), scratch, 2)
 
 
 def chain_kernel(g1h, g1l, vh, vl, lowh, lowl, g2h, g2l, *refs):
@@ -158,10 +172,9 @@
 def chain_part(g1, v, low, g2, rows):
     n = g1[0].shape[0]
     width = rows[0].shape[1]
-    half = jax.ShapeDtypeStruct((2 * n, width), BF16)
     return pl.pallas_call(
         chain_kernel,
-        out_shape=(half,) * 2,
+        out_shape=(half(2 * n, width),) * 2,
         in_specs=[VMEM] * (8 + len(rows)),
         out_specs=(VMEM,) * 2,
         scratch_shapes=[pltpu.VMEM((2 * n, width), F32)] + [pltpu.VMEM((2 * n, width), BF16)] * 2,
@@ -248,19 +261,18 @@
         return lax.ppermute(row_panel, "row", [(i, i ^ s) for i in range(n_row)])
 
     chips = tuple(range(len(HOP_ONE)))
-    ends, inner = (chips[0], chips[-1]), chips[1:-1]
     one = send(col_panel, SEND_ONE)
     two = send(col_panel, SEND_TWO)
     end = send(one, SEND_ENDS)
     middle = send(col_panel, SEND_MIDDLE)
     rows = [row_panel] + [row(s) for s in range(1, n_row)]
-    *pairs, rest = first_part(pivot)
-    g1, v, low = pairs[0:2], pairs[2:4], pairs[4:6]
-    g2 = second_part(v, low, rest)
-    y = chain_part(g1, v, low, g2, rows)
+    *g1, u, l, d = first_part(pivot)
+    vh, vl, lowh, lowl, *e = second_part(g1, u, l, d)
+    g2 = third_part(*e)
+    y = chain_part(g1, (vh, vl), (lowh, lowl), g2, rows)
     pieces = [x for mine in (col_panel, one, two) for x in (mine, exchange(mine, chips))]
     part = update_part((chips, HOP_ONE, HOP_TWO), trailing, y, pieces)
-    end_other, middle_other = exchange(end, ends), exchange(middle, inner)
+    end_other, middle_other = exchange(end, chips), exchange(middle, chips)
     return last_part(part, y, end, middle, end_other, middle_other)
 
 

time: 35 us -> 32.1 us (0.917)
  local copies, waits for them, and re-layouts: 2.2 us -> 0.02 us
  waiting for transfers between devices: 4.86 us -> 4.1 us
    ppermute x5, starting transfers between devices: 7.11 us -> 4.38 us  [exchange(): lax.ppermute(x, 'col', [(CORES * a + c, CORES * a + (c ^ 1)) for a in chi...]
    ppermute x4, starting transfers between devices: 4.26 us -> 6.86 us  [send(): lax.ppermute(x, 'col', [(CORES * a + c, CORES * b + c) for a, b in pairs...]
    unnamed x8 -> x6, local copies, waits for them, and re-layouts: 2.2 us -> 0.02 us
    ppermute x4, waiting for transfers between devices: 2.37 us -> 1.62 us  [send(): lax.ppermute(x, 'col', [(CORES * a + c, CORES * b + c) for a, b in pairs...]
    pallas_call x3 -> x4, Pallas kernels: 10.7 us -> 11 us  [the longest x3 7.2 us: kernel_call(): pl.pallas_call(body, out_shape=tuple(outs), in_specs=specs, out_specs=(VM...]
  transfers between devices with their start and end apart: 12 -> 12, of which waited for: 3 -> 2; matrix products, arithmetic and copies ran while one was open for 0% -> 0% of each run, Pallas kernels for 33% -> 37%
where the time goes in v2:
time: 32.1 us; the launch traced here: 32 us
  starting transfers between devices  14.7 us (46%)
  Pallas kernels  13 us (40%)
  waiting for transfers between devices  4.1 us (13%)
    pallas_call x3, Pallas kernels, kernel_call(): pl.pallas_call(body, out_shape=tuple(outs), in_specs=specs, out_specs=(VM...  7.2 us
    ppermute x4, starting transfers between devices, send(): lax.ppermute(x, 'col', [(CORES * a + c, CORES * b + c) for a, b in pairs...  6.86 us
    ppermute x5, starting transfers between devices, exchange(): lax.ppermute(x, 'col', [(CORES * a + c, CORES * a + (c ^ 1)) for a in chi...  4.38 us
    pallas_call x1, Pallas kernels, chain_part(): pl.pallas_call(chain_kernel, out_shape=(half(2 * n, width),) * 2, in_spec...  3.81 us
    ppermute x3, starting transfers between devices, row(): return lax.ppermute(row_panel, 'row', [(i, i ^ s) for i in range(n_row)])  3.47 us
    ppermute x3, waiting for transfers between devices, row(): return lax.ppermute(row_panel, 'row', [(i, i ^ s) for i in range(n_row)])  2.47 us
    ppermute x4, waiting for transfers between devices, send(): lax.ppermute(x, 'col', [(CORES * a + c, CORES * b + c) for a, b in pairs...  1.62 us
    pallas_call x1, Pallas kernels, last_part(): pl.pallas_call(last_kernel, out_shape=jax.ShapeDtypeStruct((m, width), F3...  1.19 us
  transfers between devices with their start and end apart: 12, of which 2 were waited for; matrix products, arithmetic and copies ran while one was open for 0% of the time, Pallas kernels for 37%

profile of v2, /device:TPU:1, one launch (start us, length us, event | category | flops | bytes accessed | tf_op | source)
XLA Modules:
  0.0 32.0 jit_solution(16126347051635910041)
XLA Ops:
  0.0 2.0 %collective-permute-start = (f32[256,256]{1,0:T(8,128)}, f32[256,256]{1,0:T(8,128)S(1)}, u32[]{:S(2)}, u32[]{:S(2)}) collective-permute-start(f32[256,256]{1,0:T(8,128)} %refs_0_.2), channel_id=1, source_target_pairs={{0,8},{8,0},{16,24},{24,16},{1,9},{9,1},{17,25},{25,17},{2,10},{10... | collective-permute-start | bytes 786440 | tf_op jit(solution)/shard_map/ppermute | solution.py:261
  2.0 2.3 %collective-permute-start.4 = (f32[512,128]{1,0:T(8,128)}, f32[512,128]{1,0:T(8,128)S(1)}, u32[]{:S(2)}, u32[]{:S(2)}) collective-permute-start(f32[512,128]{1,0:T(8,128)} %refs_0_.3), channel_id=1, source_target_pairs={{2,0},{3,1},{6,2},{7,3},{0,4},{1,5},{4,6},{5,7},{10,8},{11,9},{14,... | collective-permute-start | bytes 786440 | tf_op jit(solution)/shard_map/ppermute | solution.py:255
  4.3 1.2 %collective-permute-start.1 = (f32[256,256]{1,0:T(8,128)}, f32[256,256]{1,0:T(8,128)S(1)}, u32[]{:S(2)}, u32[]{:S(2)}) collective-permute-start(f32[256,256]{1,0:T(8,128)} %refs_0_.2), channel_id=1, source_target_pairs={{0,16},{8,24},{16,0},{24,8},{1,17},{9,25},{17,1},{25,9},{2,18},{10... | collective-permute-start | bytes 786440 | tf_op jit(solution)/shard_map/ppermute | solution.py:261
  5.6 0.2 collective-permute-start.2
  5.8 0.0 collective-permute-start.6
  5.8 2.5 %collective-permute-done.refs_1_ = f32[256,256]{1,0:T(8,128)S(1)} collective-permute-done((f32[256,256]{1,0:T(8,128)}, f32[256,256]{1,0:T(8,128)S(1)}, u32[]{:S(2)}, u32[]{:S(2)}) %collective-permute-start) | collective-permute-done | bytes 262176 | tf_op jit(solution)/shard_map/ppermute | solution.py:261
  8.2 1.6 %collective-permute-start.9 = (f32[512,128]{1,0:T(8,128)}, f32[512,128]{1,0:T(8,128)S(1)}, u32[]{:S(2)}, u32[]{:S(2)}) collective-permute-start(f32[512,128]{1,0:T(8,128)} %refs_0_.3), channel_id=1, source_target_pairs={{2,4},{3,5},{4,2},{5,3},{0,0},{1,1},{6,6},{7,7},{10,12},{11,13},{1... | collective-permute-start | bytes 786440 | tf_op jit(solution)/shard_map/ppermute | solution.py:255
  9.8 0.0 collective-permute-done.4.refs_2_
  9.8 2.9 %collective-permute-start.8 = (f32[512,128]{1,0:T(8,128)S(1)}, f32[512,128]{1,0:T(8,128)S(1)}, u32[]{:S(2)}, u32[]{:S(2)}) collective-permute-start(f32[512,128]{1,0:T(8,128)S(1)} %collective-permute-done.4.refs_2_), channel_id=1, source_target_pairs={{2,0},{3,1},{4,6},{5,7},{0,2},{1,3},{6,4},{7,5},{10,8},{11,9},{12,... | collective-permute-start | bytes 786440 | tf_op jit(solution)/shard_map/ppermute | solution.py:255
  12.8 3.2 %shard_map.46 = (bf16[512,512]{1,0:T(8,128)(2,1)S(1)}, bf16[512,512]{1,0:T(8,128)(2,1)S(1)}, f32[512,512]{1,0:T(8,128)S(1)}, f32[512,512]{1,0:T(8,128)S(1)}, f32[512,512]{1,0:T(8,128)S(1)}) custom-call(f32[1024,1024]{1,0:T(8,128)} %pivot.1), custom_call_target="tpu_custom_call" | custom-call | flops 1610612736 | bytes 4194304 | tf_op jit(solution)/shard_map/pallas_call | solution.py:93
  16.0 0.0 copy-start.1
  16.0 2.0 %shard_map.47 = (bf16[512,512]{1,0:T(8,128)(2,1)S(1)}, bf16[512,512]{1,0:T(8,128)(2,1)S(1)}, bf16[512,512]{1,0:T(8,128)(2,1)S(1)}, bf16[512,512]{1,0:T(8,128)(2,...) custom-call(bf16[512,512]{1,0:T(8,128)(2,1)S(1)} %get-tuple-element.21.g1h, ...), custom_call_target="tpu_custom_call" | custom-call | flops 1610612736 | bytes 4194304 | tf_op jit(solution)/shard_map/pallas_call | solution.py:93
  18.1 0.0 copy-start.2
  18.1 0.0 collective-permute-done.1.refs_2_
  18.1 0.0 copy-done.1
  18.1 3.3 %collective-permute-start.3 = (f32[512,128]{1,0:T(8,128)S(1)}, f32[512,128]{1,0:T(8,128)S(1)}, u32[]{:S(2)}, u32[]{:S(2)}) collective-permute-start(f32[512,128]{1,0:T(8,128)S(1)} %copy-done.1), channel_id=1, source_target_pairs={{0,1},{1,0},{2,3},{3,2},{4,5},{5,4},{6,7},{7,6},{8,9},{9,8},{10,11... | collective-permute-start | bytes 786440 | tf_op jit(solution)/shard_map/ppermute | solution.py:258
  21.4 0.0 collective-permute-done.2.refs_3_
  21.4 0.1 collective-permute-start.5
  21.5 0.0 collective-permute-done.6.refs_4_
  21.5 0.4 %collective-permute-start.7 = (f32[512,128]{1,0:T(8,128)S(1)}, f32[512,128]{1,0:T(8,128)S(1)}, u32[]{:S(2)}, u32[]{:S(2)}) collective-permute-start(f32[512,128]{1,0:T(8,128)S(1)} %collective-permute-done.6.refs_4_), channel_id=1, source_target_pairs={{0,1},{1,0},{2,3},{3,2},{4,5},{5,4},{6,7},{7,6},{8,9},{9,8},{10,11... | collective-permute-start | bytes 786440 | tf_op jit(solution)/shard_map/ppermute | solution.py:258
  21.9 0.0 collective-permute-done.9.middle
  21.9 0.1 collective-permute-start.11
  22.0 1.6 %collective-permute-done.8.end = f32[512,128]{1,0:T(8,128)S(1)} collective-permute-done((f32[512,128]{1,0:T(8,128)S(1)}, f32[512,128]{1,0:T(8,128)S(1)}, u32[]{:S(2)}, u32[]{:S(2)}) %collective-permute-start.8) | collective-permute-done | bytes 262176 | tf_op jit(solution)/shard_map/ppermute | solution.py:255
  23.6 0.5 %collective-permute-start.10 = (f32[512,128]{1,0:T(8,128)S(1)}, f32[512,128]{1,0:T(8,128)S(1)}, u32[]{:S(2)}, u32[]{:S(2)}) collective-permute-start(f32[512,128]{1,0:T(8,128)S(1)} %collective-permute-done.8.end), channel_id=1, source_target_pairs={{0,1},{1,0},{2,3},{3,2},{4,5},{5,4},{6,7},{7,6},{8,9},{9,8},{10,11... | collective-permute-start | bytes 786440 | tf_op jit(solution)/shard_map/ppermute | solution.py:258
  24.1 2.0 %shard_map.48 = (bf16[512,512]{1,0:T(8,128)(2,1)S(1)}, bf16[512,512]{1,0:T(8,128)(2,1)S(1)}) custom-call(f32[512,512]{1,0:T(8,128)S(1)} %get-tuple-element.30.e, bf16[512,512]{1,0:T(8,128)(2,1)S(1)} %get-tuple-element.31.eh, bf16[512,512]{1,0:T(8,128)(2,1)S(1)} %get-tuple-element.32.el), custom_call_target="tpu_custom_call" | custom-call | flops 1610612736 | bytes 4194304 | tf_op jit(solution)/shard_map/pallas_call | solution.py:93
  26.1 0.0 copy-start
  26.1 0.0 copy-done.2
  26.1 3.8 %chain_part.1 = (bf16[1024,256]{1,0:T(8,128)(2,1)S(1)}, bf16[1024,256]{1,0:T(8,128)(2,1)S(1)}) custom-call(bf16[512,512]{1,0:T(8,128)(2,1)S(1)} %get-tuple-element.21.g1h, bf16[512,512]{1,0:T(8,128)(2,1)S(1)} %get-tuple-element.22.g1l, bf16[512,512]{1,0:T(8,128)(2,1)S(1)} %get-tuple-element.26.vh, bf16[512,512]{1,0:T(8,128)(2,1)S(1)} %get-tuple-element.27.vl, ...), custom_call_target="tpu_custom_call" | custom-call | flops 1610612736 | bytes 6291456 | tf_op jit(solution)/shard_map/chain_part/pallas_call | solution.py:175
  29.9 0.0 collective-permute-done.3.refs_1_
  29.9 0.0 collective-permute-done.5.refs_3_
  29.9 0.0 collective-permute-done.7.refs_5_
  29.9 0.0 copy-done
  29.9 0.8 %update_part.1.part = f32[512,256]{1,0:T(8,128)S(1)} custom-call(f32[512,256]{1,0:T(8,128)S(1)} %copy-done, bf16[1024,256]{1,0:T(8,128)(2,1)S(1)} %get-tuple-element.35.yh, bf16[1024,256]{1,0:T(8,128)(2,1)S(1)} %get-tuple-element.36.yl, f32[512,128]{1,0:T(8,128)S(1)} %copy-done.1, f32[512,128]{1,0:T(8,128)S(1)} %collective-permute-done.3.refs_1_, ...), custom_call_target="tpu_custom_call" | custom-call | flops 603979776 | bytes 2621440 | tf_op jit(solution)/shard_map/update_part/pallas_call | solution.py:218
  30.8 0.0 collective-permute-done.11.middle_other
  30.8 0.0 collective-permute-done.10.end_other
  30.8 1.2 %last_part.1 = f32[512,256]{1,0:T(8,128)} custom-call(f32[512,256]{1,0:T(8,128)S(1)} %update_part.1.part, bf16[1024,256]{1,0:T(8,128)(2,1)S(1)} %get-tuple-element.35.yh, bf16[1024,256]{1,0:T(8,128)(2,1)S(1)} %get-tuple-element.36.yl, f32[512,128]{1,0:T(8,128)S(1)} %collective-permute-done.8.end, f32[512,128]{1,0:T(8,128)S(1)} %collective-permute-done.9.middle, ...), custom_call_target="tpu_custom_call" | custom-call | flops 201326592 | bytes 2097152 | tf_op jit(solution)/shard_map/last_part/pallas_call | solution.py:242
Async XLA Ops:
  0.0 8.2 %collective-permute-start = (f32[256,256]{1,0:T(8,128)}, f32[256,256]{1,0:T(8,128)S(1)}, u32[]{:S(2)}, u32[]{:S(2)}) collective-permute-start(f32[256,256]{1,0:T(8,128)} %refs_0_.2), channel_id=1, source_target_pairs={{0,8},{8,0},{16,24},{24,16},{1,9},{9,1},{17,25},{25,17},{2,10},{10... | collective-permute-start | bytes 786440 | tf_op jit(solution)/shard_map/ppermute | solution.py:261
  2.0 7.8 %collective-permute-start.4 = (f32[512,128]{1,0:T(8,128)}, f32[512,128]{1,0:T(8,128)S(1)}, u32[]{:S(2)}, u32[]{:S(2)}) collective-permute-start(f32[512,128]{1,0:T(8,128)} %refs_0_.3), channel_id=1, source_target_pairs={{2,0},{3,1},{6,2},{7,3},{0,4},{1,5},{4,6},{5,7},{10,8},{11,9},{14,... | collective-permute-start | bytes 786440 | tf_op jit(solution)/shard_map/ppermute | solution.py:255
  4.3 13.7 %collective-permute-start.1 = (f32[256,256]{1,0:T(8,128)}, f32[256,256]{1,0:T(8,128)S(1)}, u32[]{:S(2)}, u32[]{:S(2)}) collective-permute-start(f32[256,256]{1,0:T(8,128)} %refs_0_.2), channel_id=1, source_target_pairs={{0,16},{8,24},{16,0},{24,8},{1,17},{9,25},{17,1},{25,9},{2,18},{10... | collective-permute-start | bytes 786440 | tf_op jit(solution)/shard_map/ppermute | solution.py:261
  5.6 15.8 %collective-permute-start.2 = (f32[256,256]{1,0:T(8,128)}, f32[256,256]{1,0:T(8,128)S(1)}, u32[]{:S(2)}, u32[]{:S(2)}) collective-permute-start(f32[256,256]{1,0:T(8,128)} %refs_0_.2), channel_id=1, source_target_pairs={{0,24},{8,16},{16,8},{24,0},{1,25},{9,17},{17,9},{25,1},{2,26},{10... | collective-permute-start | bytes 786440 | tf_op jit(solution)/shard_map/ppermute | solution.py:261
  5.8 15.7 %collective-permute-start.6 = (f32[512,128]{1,0:T(8,128)}, f32[512,128]{1,0:T(8,128)S(1)}, u32[]{:S(2)}, u32[]{:S(2)}) collective-permute-start(f32[512,128]{1,0:T(8,128)} %refs_0_.3), channel_id=1, source_target_pairs={{4,0},{5,1},{0,2},{1,3},{6,4},{7,5},{2,6},{3,7},{12,8},{13,9},{8,1... | collective-permute-start | bytes 786440 | tf_op jit(solution)/shard_map/ppermute | solution.py:255
  8.2 13.7 %collective-permute-start.9 = (f32[512,128]{1,0:T(8,128)}, f32[512,128]{1,0:T(8,128)S(1)}, u32[]{:S(2)}, u32[]{:S(2)}) collective-permute-start(f32[512,128]{1,0:T(8,128)} %refs_0_.3), channel_id=1, source_target_pairs={{2,4},{3,5},{4,2},{5,3},{0,0},{1,1},{6,6},{7,7},{10,12},{11,13},{1... | collective-permute-start | bytes 786440 | tf_op jit(solution)/shard_map/ppermute | solution.py:255
  9.8 13.8 %collective-permute-start.8 = (f32[512,128]{1,0:T(8,128)S(1)}, f32[512,128]{1,0:T(8,128)S(1)}, u32[]{:S(2)}, u32[]{:S(2)}) collective-permute-start(f32[512,128]{1,0:T(8,128)S(1)} %collective-permute-done.4.refs_2_), channel_id=1, source_target_pairs={{2,0},{3,1},{4,6},{5,7},{0,2},{1,3},{6,4},{7,5},{10,8},{11,9},{12,... | collective-permute-start | bytes 786440 | tf_op jit(solution)/shard_map/ppermute | solution.py:255
  16.0 2.1 %copy-start.1 = (f32[512,128]{1,0:T(8,128)S(1)}, f32[512,128]{1,0:T(8,128)}, u32[]{:S(2)}) copy-start(f32[512,128]{1,0:T(8,128)} %refs_0_.3) | copy-start | bytes 786436
  18.1 8.0 %copy-start.2 = (f32[256,256]{1,0:T(8,128)S(1)}, f32[256,256]{1,0:T(8,128)}, u32[]{:S(2)}) copy-start(f32[256,256]{1,0:T(8,128)} %refs_0_.2) | copy-start | bytes 786436
  18.1 11.8 %collective-permute-start.3 = (f32[512,128]{1,0:T(8,128)S(1)}, f32[512,128]{1,0:T(8,128)S(1)}, u32[]{:S(2)}, u32[]{:S(2)}) collective-permute-start(f32[512,128]{1,0:T(8,128)S(1)} %copy-done.1), channel_id=1, source_target_pairs={{0,1},{1,0},{2,3},{3,2},{4,5},{5,4},{6,7},{7,6},{8,9},{9,8},{10,11... | collective-permute-start | bytes 786440 | tf_op jit(solution)/shard_map/ppermute | solution.py:258
  21.4 8.5 %collective-permute-start.5 = (f32[512,128]{1,0:T(8,128)S(1)}, f32[512,128]{1,0:T(8,128)S(1)}, u32[]{:S(2)}, u32[]{:S(2)}) collective-permute-start(f32[512,128]{1,0:T(8,128)S(1)} %collective-permute-done.4.refs_2_), channel_id=1, source_target_pairs={{0,1},{1,0},{2,3},{3,2},{4,5},{5,4},{6,7},{7,6},{8,9},{9,8},{10,11... | collective-permute-start | bytes 786440 | tf_op jit(solution)/shard_map/ppermute | solution.py:258
  21.5 8.4 %collective-permute-start.7 = (f32[512,128]{1,0:T(8,128)S(1)}, f32[512,128]{1,0:T(8,128)S(1)}, u32[]{:S(2)}, u32[]{:S(2)}) collective-permute-start(f32[512,128]{1,0:T(8,128)S(1)} %collective-permute-done.6.refs_4_), channel_id=1, source_target_pairs={{0,1},{1,0},{2,3},{3,2},{4,5},{5,4},{6,7},{7,6},{8,9},{9,8},{10,11... | collective-permute-start | bytes 786440 | tf_op jit(solution)/shard_map/ppermute | solution.py:258
  21.9 8.8 %collective-permute-start.11 = (f32[512,128]{1,0:T(8,128)S(1)}, f32[512,128]{1,0:T(8,128)S(1)}, u32[]{:S(2)}, u32[]{:S(2)}) collective-permute-start(f32[512,128]{1,0:T(8,128)S(1)} %collective-permute-done.9.middle), channel_id=1, source_target_pairs={{0,1},{1,0},{2,3},{3,2},{4,5},{5,4},{6,7},{7,6},{8,9},{9,8},{10,11... | collective-permute-start | bytes 786440 | tf_op jit(solution)/shard_map/ppermute | solution.py:258
  23.6 7.1 %collective-permute-start.10 = (f32[512,128]{1,0:T(8,128)S(1)}, f32[512,128]{1,0:T(8,128)S(1)}, u32[]{:S(2)}, u32[]{:S(2)}) collective-permute-start(f32[512,128]{1,0:T(8,128)S(1)} %collective-permute-done.8.end), channel_id=1, source_target_pairs={{0,1},{1,0},{2,3},{3,2},{4,5},{5,4},{6,7},{7,6},{8,9},{9,8},{10,11... | collective-permute-start | bytes 786440 | tf_op jit(solution)/shard_map/ppermute | solution.py:258
  26.1 3.9 %copy-start = (f32[512,256]{1,0:T(8,128)S(1)}, f32[512,256]{1,0:T(8,128)}, u32[]{:S(2)}) copy-start(f32[512,256]{1,0:T(8,128)} %trail.1) | copy-start | bytes 1572868

commit v3 on v2

--- a/solution.py
+++ b/solution.py
@@ -10,12 +10,13 @@
 
 F32, BF16 = jnp.float32, jnp.bfloat16
 VMEM = pl.BlockSpec(memory_space=pltpu.VMEM)
+CHUNK, LAST_CHUNK = 256, 128
 CORES = 2
 HOP_ONE, HOP_TWO, HOP_LAST = (1, 3, 0, 2), (2, 0, 3, 1), (3, 2, 1, 0)
 SEND_ONE = ((1, 0), (3, 1), (0, 2), (2, 3))
 SEND_TWO = ((2, 0), (0, 1), (3, 2), (1, 3))
 SEND_ENDS = ((1, 0), (2, 3), (0, 1), (3, 2))
-SEND_MIDDLE = ((1, 2), (2, 1), (0, 0), (3, 3))
+SEND_MIDDLE = ((1, 2), (2, 1))
 
 
 def split(x):
@@ -151,22 +152,43 @@
 
 
 def chain_kernel(g1h, g1l, vh, vl, lowh, lowl, g2h, g2l, *refs):
-    rows, (yh, yl, r, rh, rl) = refs[:-5], refs[-5:]
+    rows, (yh, yl, r, rh, rl, f, fh, fl) = refs[:-8], refs[-8:]
     n = g1h.shape[0]
     deep = rows[0].shape[0]
+    step = min(CHUNK, n)
     me = lax.axis_index("row")
     for s, piece in enumerate(rows):
         at = pl.ds(pl.multiple_of((me ^ s) * deep, deep), deep)
         x = piece[...]
         r[at, :] = x
         rh[at, :], rl[at, :] = split(x)
-    upper, lower = pl.ds(0, n), pl.ds(n, n)
-    full = lambda high, low: (high[...], low[...])
-    ya = r[upper, :] + dot3(full(g1h, g1l), (rh[upper, :], rl[upper, :]))
-    t2 = r[lower, :] - dot3(full(lowh, lowl), split(ya))
-    y2 = split(t2 + dot3(full(g2h, g2l), split(t2)))
-    yh[lower, :], yl[lower, :] = y2
-    yh[upper, :], yl[upper, :] = split(ya - dot3(full(vh, vl), y2))
+
+    def phase(left, right, finish):
+        for first in range(0, n, step):
+            at = pl.ds(first, step)
+            finish(first, at, dot3((left[0][at, :], left[1][at, :]), right))
+
+    def inner(first, at, p):
+        x = r[at, :] + p
+        f[at, :] = x
+        fh[at, :], fl[at, :] = split(x)
+
+    def residual(first, at, p):
+        x = r[pl.ds(n + first, step), :] - p
+        r[pl.ds(n + first, step), :] = x
+        rh[at, :], rl[at, :] = split(x)
+
+    def lower(first, at, p):
+        to = pl.ds(n + first, step)
+        yh[to, :], yl[to, :] = split(r[to, :] + p)
+
+    def upper(first, at, p):
+        yh[at, :], yl[at, :] = split(f[at, :] - p)
+
+    phase((g1h, g1l), (rh[pl.ds(0, n), :], rl[pl.ds(0, n), :]), inner)
+    phase((lowh, lowl), (fh[...], fl[...]), residual)
+    phase((g2h, g2l), (rh[pl.ds(0, n), :], rl[pl.ds(0, n), :]), lower)
+    phase((vh, vl), (yh[pl.ds(n, n), :], yl[pl.ds(n, n), :]), upper)
 
 
 def chain_part(g1, v, low, g2, rows):
@@ -177,7 +199,10 @@
         out_shape=(half(2 * n, width),) * 2,
         in_specs=[VMEM] * (8 + len(rows)),
         out_specs=(VMEM,) * 2,
-        scratch_shapes=[pltpu.VMEM((2 * n, width), F32)] + [pltpu.VMEM((2 * n, width), BF16)] * 2,
+        scratch_shapes=[pltpu.VMEM((2 * n, width), F32)]
+        + [pltpu.VMEM((2 * n, width), BF16)] * 2
+        + [pltpu.VMEM((n, width), F32)]
+        + [pltpu.VMEM((n, width), BF16)] * 2,
         cost_estimate=pl.CostEstimate(flops=24 * n * n * width, bytes_accessed=16 * n * (n + width), transcendentals=0),
         compiler_params=pltpu.CompilerParams(vmem_limit_bytes=16 << 20),
         name="chain_part",
@@ -204,12 +229,24 @@
     return dot3(split(both), (yh[at, :], yl[at, :]))
 
 
+def chosen(middle, end):
+    chip, _ = position()
+    return jnp.where((chip != 0) & (chip != len(HOP_LAST) - 1), middle, end)
+
+
+def narrow(shard, other, yh, yl):
+    chip, core = position()
+    wide = shard.shape[1]
+    at = pl.ds(pl.multiple_of(entry(HOP_LAST, chip) * CORES * wide + (core ^ other) * wide, wide), wide)
+    return dot3(split(shard), (yh[at, :], yl[at, :]))
+
+
 def update_kernel(tables, trail, yh, yl, *refs):
-    pieces, out = refs[:-1], refs[-1]
+    (*pieces, middle, end), out = refs[:-1], refs[-1]
     total = trail[...]
     for i, table in enumerate(tables):
         total = total - times(table, pieces[2 * i][...], pieces[2 * i + 1][...], yh, yl)
-    out[...] = total
+    out[...] = total - narrow(chosen(middle[...], end[...]), 0, yh, yl)
 
 
 def update_part(tables, trail, y, pieces):
@@ -228,12 +265,17 @@
     )(trail, *y, *pieces)
 
 
-def last_kernel(part, yh, yl, end, middle, end_other, middle_other, out):
-    chip, _ = position()
-    inner = (chip != 0) & (chip != len(HOP_LAST) - 1)
-    own = jnp.where(inner, middle[...], end[...])
-    other = jnp.where(inner, middle_other[...], end_other[...])
-    out[...] = part[...] - times(HOP_LAST, own, other, yh, yl)
+def last_kernel(part, yh, yl, middle, end, out, total, sems):
+    m = part.shape[0]
+    step = min(LAST_CHUNK, m)
+    copies = []
+    for i, first in enumerate(range(0, m, step)):
+        at = pl.ds(first, step)
+        total[at, :] = part[at, :] - narrow(chosen(middle[at, :], end[at, :]), 1, yh, yl)
+        copies.append(pltpu.make_async_copy(total.at[at, :], out.at[at, :], sems.at[i]))
+        copies[-1].start()
+    for copy in copies:
+        copy.wait()
 
 
 def last_part(part, y, *pieces):
@@ -242,25 +284,30 @@
     return pl.pallas_call(
         last_kernel,
         out_shape=jax.ShapeDtypeStruct((m, width), F32),
-        in_specs=[VMEM] * 7,
-        out_specs=VMEM,
-        cost_estimate=pl.CostEstimate(flops=12 * m * width * wide, bytes_accessed=4 * m * (2 * width + 4 * wide), transcendentals=0),
+        in_specs=[VMEM] * 5,
+        out_specs=pl.BlockSpec(memory_space=pltpu.HBM),
+        scratch_shapes=[pltpu.VMEM((m, width), F32), pltpu.SemaphoreType.DMA((-(-m // LAST_CHUNK),))],
+        cost_estimate=pl.CostEstimate(flops=6 * m * width * wide, bytes_accessed=4 * m * (2 * width + 2 * wide), transcendentals=0),
         compiler_params=pltpu.CompilerParams(vmem_limit_bytes=8 << 20),
         name="last_part",
     )(part, *y, *pieces)
 
 
 def local(n_row, pivot, col_panel, row_panel, trailing):
+    chips = tuple(range(len(HOP_ONE)))
+
     def send(x, pairs):
-        return lax.ppermute(x, "col", [(CORES * a + c, CORES * b + c) for a, b in pairs for c in range(CORES)])
-
-    def exchange(x, chips):
-        return lax.ppermute(x, "col", [(CORES * a + c, CORES * a + (c ^ 1)) for a in chips for c in range(CORES)])
+        idle = set(chips) - {a for a, _ in pairs}
+        hops = [(CORES * a + c, CORES * b + c) for a, b in pairs for c in range(CORES)]
+        swaps = [(CORES * a + c, CORES * a + (c ^ 1)) for a in sorted(idle) for c in range(CORES)]
+        return lax.ppermute(x, "col", hops + swaps)
+
+    def exchange(x):
+        return send(x, ())
 
     def row(s):
         return lax.ppermute(row_panel, "row", [(i, i ^ s) for i in range(n_row)])
 
-    chips = tuple(range(len(HOP_ONE)))
     one = send(col_panel, SEND_ONE)
     two = send(col_panel, SEND_TWO)
     end = send(one, SEND_ENDS)
@@ -270,10 +317,10 @@
     vh, vl, lowh, lowl, *e = second_part(g1, u, l, d)
     g2 = third_part(*e)
     y = chain_part(g1, (vh, vl), (lowh, lowl), g2, rows)
-    pieces = [x for mine in (col_panel, one, two) for x in (mine, exchange(mine, chips))]
-    part = update_part((chips, HOP_ONE, HOP_TWO), trailing, y, pieces)
-    end_other, middle_other = exchange(end, chips), exchange(middle, chips)
-    return last_part(part, y, end, middle, end_other, middle_other)
+    pieces = [x for mine in (col_panel, one, two) for x in (mine, exchange(mine))]
+    part = update_part((chips, HOP_ONE, HOP_TWO), trailing, y, pieces + [middle, end])
+    others = exchange(middle), exchange(end)
+    return last_part(part, y, *others)
 
 
 def exact(left, right):

time: 32.1 us -> 30.4 us (0.947)
  Pallas kernels: 13 us -> 11.8 us
  starting transfers between devices: 14.7 us -> 13.9 us
    pallas_call x1, Pallas kernels: 3.81 us -> 2.52 us  [chain_part(): pl.pallas_call(chain_kernel, out_shape=(half(2 * n, width),) * 2, in_spec...]
    ppermute x9, starting transfers between devices: 11.2 us -> 10.4 us  [send(): return lax.ppermute(x, 'col', hops + swaps)]
  transfers between devices with their start and end apart: 12 -> 12, of which waited for: 2 -> 3; matrix products, arithmetic and copies ran while one was open for 0% -> 0% of each run, Pallas kernels for 37% -> 35%
where the time goes in v3:
time: 30.4 us; the launch traced here: 30.3 us
  starting transfers between devices  13.9 us (46%)
  Pallas kernels  11.8 us (39%)
  waiting for transfers between devices  4.41 us (15%)
    ppermute x9, starting transfers between devices, send(): return lax.ppermute(x, 'col', hops + swaps)  10.4 us
    pallas_call x3, Pallas kernels, kernel_call(): pl.pallas_call(body, out_shape=tuple(outs), in_specs=specs, out_specs=(VM...  7.2 us
    ppermute x3, starting transfers between devices, row(): return lax.ppermute(row_panel, 'row', [(i, i ^ s) for i in range(n_row)])  3.47 us
    ppermute x3, waiting for transfers between devices, row(): return lax.ppermute(row_panel, 'row', [(i, i ^ s) for i in range(n_row)])  2.63 us
    pallas_call x1, Pallas kernels, chain_part(): pl.pallas_call(chain_kernel, out_shape=(half(2 * n, width),) * 2, in_spec...  2.52 us
    ppermute x9, waiting for transfers between devices, send(): return lax.ppermute(x, 'col', hops + swaps)  1.78 us
    pallas_call x1, Pallas kernels, last_part(): pl.pallas_call(last_kernel, out_shape=jax.ShapeDtypeStruct((m, width), F3...  1.11 us
    pallas_call x1, Pallas kernels, update_part(): pl.pallas_call(functools.partial(update_kernel, tables), out_shape=jax.Sh...  1 us
  transfers between devices with their start and end apart: 12, of which 3 were waited for; matrix products, arithmetic and copies ran while one was open for 0% of the time, Pallas kernels for 35%

profile of v3, /device:TPU:1, one launch (start us, length us, event | category | flops | bytes accessed | tf_op | source)
XLA Modules:
  0.0 30.3 jit_solution(16287634907199034978)
XLA Ops:
  0.0 2.0 %collective-permute-start = (f32[256,256]{1,0:T(8,128)}, f32[256,256]{1,0:T(8,128)S(1)}, u32[]{:S(2)}, u32[]{:S(2)}) collective-permute-start(f32[256,256]{1,0:T(8,128)} %refs_0_.2), channel_id=1, source_target_pairs={{0,8},{8,0},{16,24},{24,16},{1,9},{9,1},{17,25},{25,17},{2,10},{10... | collective-permute-start | bytes 786440 | tf_op jit(solution)/shard_map/ppermute | solution.py:309
  2.0 2.3 %collective-permute-start.4 = (f32[512,128]{1,0:T(8,128)}, f32[512,128]{1,0:T(8,128)S(1)}, u32[]{:S(2)}, u32[]{:S(2)}) collective-permute-start(f32[512,128]{1,0:T(8,128)} %refs_0_.3), channel_id=1, source_target_pairs={{2,0},{3,1},{6,2},{7,3},{0,4},{1,5},{4,6},{5,7},{10,8},{11,9},{14,... | collective-permute-start | bytes 786440 | tf_op jit(solution)/shard_map/ppermute | solution.py:303
  4.3 1.2 %collective-permute-start.1 = (f32[256,256]{1,0:T(8,128)}, f32[256,256]{1,0:T(8,128)S(1)}, u32[]{:S(2)}, u32[]{:S(2)}) collective-permute-start(f32[256,256]{1,0:T(8,128)} %refs_0_.2), channel_id=1, source_target_pairs={{0,16},{8,24},{16,0},{24,8},{1,17},{9,25},{17,1},{25,9},{2,18},{10... | collective-permute-start | bytes 786440 | tf_op jit(solution)/shard_map/ppermute | solution.py:309
  5.6 0.2 collective-permute-start.2
  5.8 0.0 collective-permute-start.6
  5.8 2.5 %collective-permute-done.refs_1_ = f32[256,256]{1,0:T(8,128)S(1)} collective-permute-done((f32[256,256]{1,0:T(8,128)}, f32[256,256]{1,0:T(8,128)S(1)}, u32[]{:S(2)}, u32[]{:S(2)}) %collective-permute-start) | collective-permute-done | bytes 262176 | tf_op jit(solution)/shard_map/ppermute | solution.py:309
  8.2 1.9 %collective-permute-start.8 = (f32[512,128]{1,0:T(8,128)}, f32[512,128]{1,0:T(8,128)S(1)}, u32[]{:S(2)}, u32[]{:S(2)}) collective-permute-start(f32[512,128]{1,0:T(8,128)} %refs_0_.3), channel_id=1, source_target_pairs={{2,4},{3,5},{4,2},{5,3},{0,1},{1,0},{6,7},{7,6},{10,12},{11,13},{1... | collective-permute-start | bytes 786440 | tf_op jit(solution)/shard_map/ppermute | solution.py:303
  10.2 0.0 collective-permute-done.4.refs_2_
  10.2 1.2 %collective-permute-start.9 = (f32[512,128]{1,0:T(8,128)S(1)}, f32[512,128]{1,0:T(8,128)S(1)}, u32[]{:S(2)}, u32[]{:S(2)}) collective-permute-start(f32[512,128]{1,0:T(8,128)S(1)} %collective-permute-done.4.refs_2_), channel_id=1, source_target_pairs={{2,0},{3,1},{4,6},{5,7},{0,2},{1,3},{6,4},{7,5},{10,8},{11,9},{12,... | collective-permute-start | bytes 786440 | tf_op jit(solution)/shard_map/ppermute | solution.py:303
  11.3 3.2 %shard_map.46 = (bf16[512,512]{1,0:T(8,128)(2,1)S(1)}, bf16[512,512]{1,0:T(8,128)(2,1)S(1)}, f32[512,512]{1,0:T(8,128)S(1)}, f32[512,512]{1,0:T(8,128)S(1)}, f32[512,512]{1,0:T(8,128)S(1)}) custom-call(f32[1024,1024]{1,0:T(8,128)} %pivot.1), custom_call_target="tpu_custom_call" | custom-call | flops 1610612736 | bytes 4194304 | tf_op jit(solution)/shard_map/pallas_call | solution.py:94
  14.6 0.0 copy-start.1
  14.6 2.0 %shard_map.47 = (bf16[512,512]{1,0:T(8,128)(2,1)S(1)}, bf16[512,512]{1,0:T(8,128)(2,1)S(1)}, bf16[512,512]{1,0:T(8,128)(2,1)S(1)}, bf16[512,512]{1,0:T(8,128)(2,...) custom-call(bf16[512,512]{1,0:T(8,128)(2,1)S(1)} %get-tuple-element.21.g1h, ...), custom_call_target="tpu_custom_call" | custom-call | flops 1610612736 | bytes 4194304 | tf_op jit(solution)/shard_map/pallas_call | solution.py:94
  16.6 0.0 copy-start.2
  16.6 0.2 collective-permute-done.1.refs_2_
  16.8 0.0 copy-done.1
  16.8 3.4 %collective-permute-start.3 = (f32[512,128]{1,0:T(8,128)S(1)}, f32[512,128]{1,0:T(8,128)S(1)}, u32[]{:S(2)}, u32[]{:S(2)}) collective-permute-start(f32[512,128]{1,0:T(8,128)S(1)} %copy-done.1), channel_id=1, source_target_pairs={{0,1},{1,0},{2,3},{3,2},{4,5},{5,4},{6,7},{7,6},{8,9},{9,8},{10,11... | collective-permute-start | bytes 786440 | tf_op jit(solution)/shard_map/ppermute | solution.py:303
  20.2 0.0 collective-permute-done.2.refs_3_
  20.2 0.1 collective-permute-start.5
  20.3 0.0 collective-permute-done.6.refs_4_
  20.3 0.4 %collective-permute-start.7 = (f32[512,128]{1,0:T(8,128)S(1)}, f32[512,128]{1,0:T(8,128)S(1)}, u32[]{:S(2)}, u32[]{:S(2)}) collective-permute-start(f32[512,128]{1,0:T(8,128)S(1)} %collective-permute-done.6.refs_4_), channel_id=1, source_target_pairs={{0,1},{1,0},{2,3},{3,2},{4,5},{5,4},{6,7},{7,6},{8,9},{9,8},{10,11... | collective-permute-start | bytes 786440 | tf_op jit(solution)/shard_map/ppermute | solution.py:303
  20.7 0.0 collective-permute-done.8.refs_6_
  20.7 0.1 collective-permute-start.10
  20.8 1.8 %collective-permute-done.9.refs_7_ = f32[512,128]{1,0:T(8,128)S(1)} collective-permute-done((f32[512,128]{1,0:T(8,128)S(1)}, f32[512,128]{1,0:T(8,128)S(1)}, u32[]{:S(2)}, u32[]{:S(2)}) %collective-permute-start.9) | collective-permute-done | bytes 262176 | tf_op jit(solution)/shard_map/ppermute | solution.py:303
  22.6 1.0 %collective-permute-start.11 = (f32[512,128]{1,0:T(8,128)S(1)}, f32[512,128]{1,0:T(8,128)S(1)}, u32[]{:S(2)}, u32[]{:S(2)}) collective-permute-start(f32[512,128]{1,0:T(8,128)S(1)} %collective-permute-done.9.refs_7_), channel_id=1, source_target_pairs={{0,1},{1,0},{2,3},{3,2},{4,5},{5,4},{6,7},{7,6},{8,9},{9,8},{10,11... | collective-permute-start | bytes 786440 | tf_op jit(solution)/shard_map/ppermute | solution.py:303
  23.6 2.0 %shard_map.48 = (bf16[512,512]{1,0:T(8,128)(2,1)S(1)}, bf16[512,512]{1,0:T(8,128)(2,1)S(1)}) custom-call(f32[512,512]{1,0:T(8,128)S(1)} %get-tuple-element.30.e, bf16[512,512]{1,0:T(8,128)(2,1)S(1)} %get-tuple-element.31.eh, bf16[512,512]{1,0:T(8,128)(2,1)S(1)} %get-tuple-element.32.el), custom_call_target="tpu_custom_call" | custom-call | flops 1610612736 | bytes 4194304 | tf_op jit(solution)/shard_map/pallas_call | solution.py:94
  25.6 0.0 copy-start
  25.6 0.0 copy-done.2
  25.6 2.5 %chain_part.1 = (bf16[1024,256]{1,0:T(8,128)(2,1)S(1)}, bf16[1024,256]{1,0:T(8,128)(2,1)S(1)}) custom-call(bf16[512,512]{1,0:T(8,128)(2,1)S(1)} %get-tuple-element.21.g1h, bf16[512,512]{1,0:T(8,128)(2,1)S(1)} %get-tuple-element.22.g1l, bf16[512,512]{1,0:T(8,128)(2,1)S(1)} %get-tuple-element.26.vh, bf16[512,512]{1,0:T(8,128)(2,1)S(1)} %get-tuple-element.27.vl, ...), custom_call_target="tpu_custom_call" | custom-call | flops 1610612736 | bytes 6291456 | tf_op jit(solution)/shard_map/chain_part/pallas_call | solution.py:197
  28.1 0.0 collective-permute-done.3.refs_1_
  28.1 0.0 collective-permute-done.5.refs_3_
  28.1 0.0 collective-permute-done.7.refs_5_
  28.1 0.0 copy-done
  28.1 1.0 %update_part.1.part = f32[512,256]{1,0:T(8,128)S(1)} custom-call(f32[512,256]{1,0:T(8,128)S(1)} %copy-done, bf16[1024,256]{1,0:T(8,128)(2,1)S(1)} %get-tuple-element.35.yh, bf16[1024,256]{1,0:T(8,128)(2,1)S(1)} %get-tuple-element.36.yl, f32[512,128]{1,0:T(8,128)S(1)} %copy-done.1, f32[512,128]{1,0:T(8,128)S(1)} %collective-permute-done.3.refs_1_, ...), custom_call_target="tpu_custom_call" | custom-call | flops 805306368 | bytes 3145728 | tf_op jit(solution)/shard_map/update_part/pallas_call | solution.py:255
  29.2 0.0 collective-permute-done.10.middle
  29.2 0.0 collective-permute-done.11.end
  29.2 1.1 %last_part.1 = f32[512,256]{1,0:T(8,128)} custom-call(f32[512,256]{1,0:T(8,128)S(1)} %update_part.1.part, bf16[1024,256]{1,0:T(8,128)(2,1)S(1)} %get-tuple-element.35.yh, bf16[1024,256]{1,0:T(8,128)(2,1)S(1)} %get-tuple-element.36.yl, f32[512,128]{1,0:T(8,128)S(1)} %collective-permute-done.10.middle, f32[512,128]{1,0:T(8,128)S(1)} %collective-permute-done.11.end), custom_call_target="tpu_custom_call" | custom-call | flops 100663296 | bytes 1572864 | tf_op jit(solution)/shard_map/last_part/pallas_call | solution.py:284
Async XLA Ops:
  0.0 8.2 %collective-permute-start = (f32[256,256]{1,0:T(8,128)}, f32[256,256]{1,0:T(8,128)S(1)}, u32[]{:S(2)}, u32[]{:S(2)}) collective-permute-start(f32[256,256]{1,0:T(8,128)} %refs_0_.2), channel_id=1, source_target_pairs={{0,8},{8,0},{16,24},{24,16},{1,9},{9,1},{17,25},{25,17},{2,10},{10... | collective-permute-start | bytes 786440 | tf_op jit(solution)/shard_map/ppermute | solution.py:309
  2.0 8.1 %collective-permute-start.4 = (f32[512,128]{1,0:T(8,128)}, f32[512,128]{1,0:T(8,128)S(1)}, u32[]{:S(2)}, u32[]{:S(2)}) collective-permute-start(f32[512,128]{1,0:T(8,128)} %refs_0_.3), channel_id=1, source_target_pairs={{2,0},{3,1},{6,2},{7,3},{0,4},{1,5},{4,6},{5,7},{10,8},{11,9},{14,... | collective-permute-start | bytes 786440 | tf_op jit(solution)/shard_map/ppermute | solution.py:303
  4.3 12.5 %collective-permute-start.1 = (f32[256,256]{1,0:T(8,128)}, f32[256,256]{1,0:T(8,128)S(1)}, u32[]{:S(2)}, u32[]{:S(2)}) collective-permute-start(f32[256,256]{1,0:T(8,128)} %refs_0_.2), channel_id=1, source_target_pairs={{0,16},{8,24},{16,0},{24,8},{1,17},{9,25},{17,1},{25,9},{2,18},{10... | collective-permute-start | bytes 786440 | tf_op jit(solution)/shard_map/ppermute | solution.py:309
  5.6 14.6 %collective-permute-start.2 = (f32[256,256]{1,0:T(8,128)}, f32[256,256]{1,0:T(8,128)S(1)}, u32[]{:S(2)}, u32[]{:S(2)}) collective-permute-start(f32[256,256]{1,0:T(8,128)} %refs_0_.2), channel_id=1, source_target_pairs={{0,24},{8,16},{16,8},{24,0},{1,25},{9,17},{17,9},{25,1},{2,26},{10... | collective-permute-start | bytes 786440 | tf_op jit(solution)/shard_map/ppermute | solution.py:309
  5.8 14.5 %collective-permute-start.6 = (f32[512,128]{1,0:T(8,128)}, f32[512,128]{1,0:T(8,128)S(1)}, u32[]{:S(2)}, u32[]{:S(2)}) collective-permute-start(f32[512,128]{1,0:T(8,128)} %refs_0_.3), channel_id=1, source_target_pairs={{4,0},{5,1},{0,2},{1,3},{6,4},{7,5},{2,6},{3,7},{12,8},{13,9},{8,1... | collective-permute-start | bytes 786440 | tf_op jit(solution)/shard_map/ppermute | solution.py:303
  8.2 12.5 %collective-permute-start.8 = (f32[512,128]{1,0:T(8,128)}, f32[512,128]{1,0:T(8,128)S(1)}, u32[]{:S(2)}, u32[]{:S(2)}) collective-permute-start(f32[512,128]{1,0:T(8,128)} %refs_0_.3), channel_id=1, source_target_pairs={{2,4},{3,5},{4,2},{5,3},{0,1},{1,0},{6,7},{7,6},{10,12},{11,13},{1... | collective-permute-start | bytes 786440 | tf_op jit(solution)/shard_map/ppermute | solution.py:303
  10.2 12.4 %collective-permute-start.9 = (f32[512,128]{1,0:T(8,128)S(1)}, f32[512,128]{1,0:T(8,128)S(1)}, u32[]{:S(2)}, u32[]{:S(2)}) collective-permute-start(f32[512,128]{1,0:T(8,128)S(1)} %collective-permute-done.4.refs_2_), channel_id=1, source_target_pairs={{2,0},{3,1},{4,6},{5,7},{0,2},{1,3},{6,4},{7,5},{10,8},{11,9},{12,... | collective-permute-start | bytes 786440 | tf_op jit(solution)/shard_map/ppermute | solution.py:303
  14.6 2.2 %copy-start.1 = (f32[512,128]{1,0:T(8,128)S(1)}, f32[512,128]{1,0:T(8,128)}, u32[]{:S(2)}) copy-start(f32[512,128]{1,0:T(8,128)} %refs_0_.3) | copy-start | bytes 786436
  16.6 9.0 %copy-start.2 = (f32[256,256]{1,0:T(8,128)S(1)}, f32[256,256]{1,0:T(8,128)}, u32[]{:S(2)}) copy-start(f32[256,256]{1,0:T(8,128)} %refs_0_.2) | copy-start | bytes 786436
  16.8 11.3 %collective-permute-start.3 = (f32[512,128]{1,0:T(8,128)S(1)}, f32[512,128]{1,0:T(8,128)S(1)}, u32[]{:S(2)}, u32[]{:S(2)}) collective-permute-start(f32[512,128]{1,0:T(8,128)S(1)} %copy-done.1), channel_id=1, source_target_pairs={{0,1},{1,0},{2,3},{3,2},{4,5},{5,4},{6,7},{7,6},{8,9},{9,8},{10,11... | collective-permute-start | bytes 786440 | tf_op jit(solution)/shard_map/ppermute | solution.py:303
  20.2 7.9 %collective-permute-start.5 = (f32[512,128]{1,0:T(8,128)S(1)}, f32[512,128]{1,0:T(8,128)S(1)}, u32[]{:S(2)}, u32[]{:S(2)}) collective-permute-start(f32[512,128]{1,0:T(8,128)S(1)} %collective-permute-done.4.refs_2_), channel_id=1, source_target_pairs={{0,1},{1,0},{2,3},{3,2},{4,5},{5,4},{6,7},{7,6},{8,9},{9,8},{10,11... | collective-permute-start | bytes 786440 | tf_op jit(solution)/shard_map/ppermute | solution.py:303
  20.3 7.8 %collective-permute-start.7 = (f32[512,128]{1,0:T(8,128)S(1)}, f32[512,128]{1,0:T(8,128)S(1)}, u32[]{:S(2)}, u32[]{:S(2)}) collective-permute-start(f32[512,128]{1,0:T(8,128)S(1)} %collective-permute-done.6.refs_4_), channel_id=1, source_target_pairs={{0,1},{1,0},{2,3},{3,2},{4,5},{5,4},{6,7},{7,6},{8,9},{9,8},{10,11... | collective-permute-start | bytes 786440 | tf_op jit(solution)/shard_map/ppermute | solution.py:303
  20.7 8.4 %collective-permute-start.10 = (f32[512,128]{1,0:T(8,128)S(1)}, f32[512,128]{1,0:T(8,128)S(1)}, u32[]{:S(2)}, u32[]{:S(2)}) collective-permute-start(f32[512,128]{1,0:T(8,128)S(1)} %collective-permute-done.8.refs_6_), channel_id=1, source_target_pairs={{0,1},{1,0},{2,3},{3,2},{4,5},{5,4},{6,7},{7,6},{8,9},{9,8},{10,11... | collective-permute-start | bytes 786440 | tf_op jit(solution)/shard_map/ppermute | solution.py:303
  22.6 6.6 %collective-permute-start.11 = (f32[512,128]{1,0:T(8,128)S(1)}, f32[512,128]{1,0:T(8,128)S(1)}, u32[]{:S(2)}, u32[]{:S(2)}) collective-permute-start(f32[512,128]{1,0:T(8,128)S(1)} %collective-permute-done.9.refs_7_), channel_id=1, source_target_pairs={{0,1},{1,0},{2,3},{3,2},{4,5},{5,4},{6,7},{7,6},{8,9},{9,8},{10,11... | collective-permute-start | bytes 786440 | tf_op jit(solution)/shard_map/ppermute | solution.py:303
  25.6 2.6 %copy-start = (f32[512,256]{1,0:T(8,128)S(1)}, f32[512,256]{1,0:T(8,128)}, u32[]{:S(2)}) copy-start(f32[512,256]{1,0:T(8,128)} %trail.1) | copy-start | bytes 1572868

commit v4 on v3

--- a/solution.py
+++ b/solution.py
@@ -10,7 +10,7 @@
 
 F32, BF16 = jnp.float32, jnp.bfloat16
 VMEM = pl.BlockSpec(memory_space=pltpu.VMEM)
-CHUNK, LAST_CHUNK = 256, 128
+CHUNK, TAIL = 256, 64
 CORES = 2
 HOP_ONE, HOP_TWO, HOP_LAST = (1, 3, 0, 2), (2, 0, 3, 1), (3, 2, 1, 0)
 SEND_ONE = ((1, 0), (3, 1), (0, 2), (2, 3))
@@ -118,8 +118,9 @@
     return kernel_call(first_kernel, "first_part", outs, (pivot,), scratch, 2)
 
 
-def second_kernel(g1h, g1l, u, l, d, vh, vl, lowh, lowl, e, eh, el, uh, ul):
+def second_kernel(g1h, g1l, u, l, d, shard, vh, vl, lowh, lowl, e, eh, el, head, uh, ul):
     n = u.shape[0]
+    head[...] = shard[pl.ds(0, head.shape[0]), :]
     g1, v, low, up = (g1h, g1l), (vh, vl), (lowh, lowl), (uh, ul)
     each(n, lambda cols, _: put(up, cols, u[:, cols]))
     each(n, lambda cols, _: put(v, cols, u[:, cols] + product(g1, up, cols)))
@@ -133,22 +134,26 @@
     each(n, residual)
 
 
-def second_part(g1, u, l, d):
+def second_part(g1, u, l, d, shard):
     n = u.shape[0]
-    outs = [half(n, n)] * 4 + [single(n, n)] + [half(n, n)] * 2
-    return kernel_call(second_kernel, "second_part", outs, (*g1, u, l, d), [pltpu.VMEM((n, n), BF16)] * 2, 2)
-
-
-def third_kernel(e, eh, el, g2h, g2l, x, fh, fl):
+    m, wide = shard.shape
+    outs = [half(n, n)] * 4 + [single(n, n)] + [half(n, n)] * 2 + [single(m - TAIL, wide)]
+    return kernel_call(second_kernel, "second_part", outs, (*g1, u, l, d, shard), [pltpu.VMEM((n, n), BF16)] * 2, 2)
+
+
+def third_kernel(e, eh, el, own, other, g2h, g2l, tails, x, fh, fl):
     n = e.shape[0]
+    for i, shard in enumerate((own, other)):
+        tails[pl.ds(i * TAIL, TAIL), :] = shard[pl.ds(shard.shape[0] - TAIL, TAIL), :]
     x[...] = e[...]
     powers(n, x, (eh, el), (fh, fl), (g2h, g2l))
 
 
-def third_part(e, eh, el):
-    n = e.shape[0]
+def third_part(e, own, other):
+    n = e[0].shape[0]
+    outs = [half(n, n)] * 2 + [single(2 * TAIL, own.shape[1])]
     scratch = [pltpu.VMEM((n, n), F32)] + [pltpu.VMEM((n, n), BF16)] * 2
-    return kernel_call(third_kernel, "third_part", [half(n, n)] * 2, (e, eh, el), scratch, 2)
+    return kernel_call(third_kernel, "third_part", outs, (*e, own, other), scratch, 2)
 
 
 def chain_kernel(g1h, g1l, vh, vl, lowh, lowl, g2h, g2l, *refs):
@@ -214,6 +219,11 @@
     return me // CORES, me % CORES
 
 
+def at_end():
+    chip, _ = position()
+    return (chip == 0) | (chip == len(HOP_LAST) - 1)
+
+
 def entry(table, index):
     value = jnp.int32(table[0])
     for i, x in enumerate(table[1:], 1):
@@ -230,8 +240,7 @@
 
 
 def chosen(middle, end):
-    chip, _ = position()
-    return jnp.where((chip != 0) & (chip != len(HOP_LAST) - 1), middle, end)
+    return jnp.where(at_end(), end, middle)
 
 
 def narrow(shard, other, yh, yl):
@@ -242,11 +251,13 @@
 
 
 def update_kernel(tables, trail, yh, yl, *refs):
-    (*pieces, middle, end), out = refs[:-1], refs[-1]
+    (*pieces, middle, head), out = refs[:-1], refs[-1]
+    rows = pl.ds(0, head.shape[0])
     total = trail[...]
     for i, table in enumerate(tables):
         total = total - times(table, pieces[2 * i][...], pieces[2 * i + 1][...], yh, yl)
-    out[...] = total - narrow(chosen(middle[...], end[...]), 0, yh, yl)
+    out[...] = total
+    out[rows, :] = out[rows, :] - narrow(chosen(middle[rows, :], head[...]), 0, yh, yl)
 
 
 def update_part(tables, trail, y, pieces):
@@ -265,13 +276,16 @@
     )(trail, *y, *pieces)
 
 
-def last_kernel(part, yh, yl, middle, end, out, total, sems):
-    m = part.shape[0]
-    step = min(LAST_CHUNK, m)
+def last_kernel(blocks, part, yh, yl, middle, middle_other, head_other, tails, out, total, sems):
+    rows = head_other.shape[0]
     copies = []
-    for i, first in enumerate(range(0, m, step)):
-        at = pl.ds(first, step)
-        total[at, :] = part[at, :] - narrow(chosen(middle[at, :], end[at, :]), 1, yh, yl)
+    for i, (first, size) in enumerate(blocks):
+        at = pl.ds(first, size)
+        if first < rows:
+            x = narrow(chosen(middle_other[at, :], head_other[at, :]), 1, yh, yl)
+        else:
+            x = times(HOP_LAST, chosen(middle[at, :], tails[:TAIL, :]), chosen(middle_other[at, :], tails[TAIL:, :]), yh, yl)
+        total[at, :] = part[at, :] - x
         copies.append(pltpu.make_async_copy(total.at[at, :], out.at[at, :], sems.at[i]))
         copies[-1].start()
     for copy in copies:
@@ -280,13 +294,15 @@
 
 def last_part(part, y, *pieces):
     m, width = part.shape
-    wide = pieces[0].shape[1]
+    rows, wide = pieces[2].shape
+    cuts = list(range(0, rows, CHUNK // 2)) + [rows, m]
+    blocks = [(first, end - first) for first, end in zip(cuts, cuts[1:])]
     return pl.pallas_call(
-        last_kernel,
+        functools.partial(last_kernel, blocks),
         out_shape=jax.ShapeDtypeStruct((m, width), F32),
-        in_specs=[VMEM] * 5,
+        in_specs=[VMEM] * 7,
         out_specs=pl.BlockSpec(memory_space=pltpu.HBM),
-        scratch_shapes=[pltpu.VMEM((m, width), F32), pltpu.SemaphoreType.DMA((-(-m // LAST_CHUNK),))],
+        scratch_shapes=[pltpu.VMEM((m, width), F32), pltpu.SemaphoreType.DMA((len(blocks),))],
         cost_estimate=pl.CostEstimate(flops=6 * m * width * wide, bytes_accessed=4 * m * (2 * width + 2 * wide), transcendentals=0),
         compiler_params=pltpu.CompilerParams(vmem_limit_bytes=8 << 20),
         name="last_part",
@@ -310,17 +326,19 @@
 
     one = send(col_panel, SEND_ONE)
     two = send(col_panel, SEND_TWO)
-    end = send(one, SEND_ENDS)
     middle = send(col_panel, SEND_MIDDLE)
     rows = [row_panel] + [row(s) for s in range(1, n_row)]
+    one_other = exchange(one)
     *g1, u, l, d = first_part(pivot)
-    vh, vl, lowh, lowl, *e = second_part(g1, u, l, d)
-    g2 = third_part(*e)
+    vh, vl, lowh, lowl, *e, head = second_part(g1, u, l, d, one)
+    head = send(head, SEND_ENDS)
+    *g2, tails = third_part(e, one, one_other)
+    tails = send(tails, SEND_ENDS)
     y = chain_part(g1, (vh, vl), (lowh, lowl), g2, rows)
-    pieces = [x for mine in (col_panel, one, two) for x in (mine, exchange(mine))]
-    part = update_part((chips, HOP_ONE, HOP_TWO), trailing, y, pieces + [middle, end])
-    others = exchange(middle), exchange(end)
-    return last_part(part, y, *others)
+    pieces = [col_panel, exchange(col_panel), one, one_other, two, exchange(two)]
+    part = update_part((chips, HOP_ONE, HOP_TWO), trailing, y, pieces + [middle, head])
+    others = exchange(middle), exchange(head)
+    return last_part(part, y, middle, *others, tails)
 
 
 def exact(left, right):

time: 30.4 us -> 35.9 us (1.18)
  the two profiles are of different devices: /device:TPU:1 before, /device:TPU:0 now
where the time goes in v4:
time: 35.9 us; the launch traced here: 35.7 us
  starting transfers between devices  13.2 us (37%)
  Pallas kernels  11.8 us (33%)
  waiting for transfers between devices  10.5 us (29%)
    ppermute x10, waiting for transfers between devices, send(): return lax.ppermute(x, 'col', hops + swaps)  10.5 us
    ppermute x10, starting transfers between devices, send(): return lax.ppermute(x, 'col', hops + swaps)  7.75 us
    pallas_call x3, Pallas kernels, kernel_call(): pl.pallas_call(body, out_shape=tuple(outs), in_specs=specs, out_specs=(VM...  7.22 us
    ppermute x3, starting transfers between devices, row(): return lax.ppermute(row_panel, 'row', [(i, i ^ s) for i in range(n_row)])  5.46 us
    pallas_call x1, Pallas kernels, chain_part(): pl.pallas_call(chain_kernel, out_shape=(half(2 * n, width),) * 2, in_spec...  2.52 us
    pallas_call x1, Pallas kernels, last_part(): pl.pallas_call(functools.partial(last_kernel, blocks), out_shape=jax.Shap...  1.11 us
    pallas_call x1, Pallas kernels, update_part(): pl.pallas_call(functools.partial(update_kernel, tables), out_shape=jax.Sh...  0.98 us
  transfers between devices with their start and end apart: 13, of which 3 were waited for; matrix products, arithmetic and copies ran while one was open for 0% of the time, Pallas kernels for 30%

profile of v4, /device:TPU:0, one launch (start us, length us, event | category | flops | bytes accessed | tf_op | source)
XLA Modules:
  0.0 35.7 jit_solution(6113719542148373892)
XLA Ops:
  0.0 4.1 %collective-permute-start = (f32[512,128]{1,0:T(8,128)}, f32[512,128]{1,0:T(8,128)S(1)}, u32[]{:S(2)}, u32[]{:S(2)}) collective-permute-start(f32[512,128]{1,0:T(8,128)} %refs_0_.3), channel_id=1, source_target_pairs={{2,0},{3,1},{6,2},{7,3},{0,4},{1,5},{4,6},{5,7},{10,8},{11,9},{14,... | collective-permute-start | bytes 786440 | tf_op jit(solution)/shard_map/ppermute | solution.py:319
  4.1 1.5 %collective-permute-start.2 = (f32[256,256]{1,0:T(8,128)}, f32[256,256]{1,0:T(8,128)S(1)}, u32[]{:S(2)}, u32[]{:S(2)}) collective-permute-start(f32[256,256]{1,0:T(8,128)} %refs_0_.2), channel_id=1, source_target_pairs={{0,8},{8,0},{16,24},{24,16},{1,9},{9,1},{17,25},{25,17},{2,10},{10... | collective-permute-start | bytes 786440 | tf_op jit(solution)/shard_map/ppermute | solution.py:325
  5.6 1.5 %collective-permute-start.3 = (f32[256,256]{1,0:T(8,128)}, f32[256,256]{1,0:T(8,128)S(1)}, u32[]{:S(2)}, u32[]{:S(2)}) collective-permute-start(f32[256,256]{1,0:T(8,128)} %refs_0_.2), channel_id=1, source_target_pairs={{0,16},{8,24},{16,0},{24,8},{1,17},{9,25},{17,1},{25,9},{2,18},{10... | collective-permute-start | bytes 786440 | tf_op jit(solution)/shard_map/ppermute | solution.py:325
  7.1 0.0 collective-permute-start.8
  7.1 2.1 %collective-permute-start.6 = (f32[512,128]{1,0:T(8,128)}, f32[512,128]{1,0:T(8,128)S(1)}, u32[]{:S(2)}, u32[]{:S(2)}) collective-permute-start(f32[512,128]{1,0:T(8,128)} %refs_0_.3), channel_id=1, source_target_pairs={{4,0},{5,1},{0,2},{1,3},{6,4},{7,5},{2,6},{3,7},{12,8},{13,9},{8,1... | collective-permute-start | bytes 786440 | tf_op jit(solution)/shard_map/ppermute | solution.py:319
  9.2 3.2 %shard_map.46 = (bf16[512,512]{1,0:T(8,128)(2,1)S(1)}, bf16[512,512]{1,0:T(8,128)(2,1)S(1)}, f32[512,512]{1,0:T(8,128)S(1)}, f32[512,512]{1,0:T(8,128)S(1)}, f32[512,512]{1,0:T(8,128)S(1)}) custom-call(f32[1024,1024]{1,0:T(8,128)} %pivot.1), custom_call_target="tpu_custom_call" | custom-call | flops 1610612736 | bytes 4194304 | tf_op jit(solution)/shard_map/pallas_call | solution.py:94
  12.4 0.0 copy-start.2
  12.5 0.0 copy-start.1
  12.5 0.0 collective-permute-done.shard.own.refs_2_
  12.5 0.1 collective-permute-start.1
  12.6 2.0 %shard_map.47 = (bf16[512,512]{1,0:T(8,128)(2,1)S(1)}, bf16[512,512]{1,0:T(8,128)(2,1)S(1)}, bf16[512,512]{1,0:T(8,128)(2,1)S(1)}, bf16[512,512]{1,0:T(8,128)(2,...) custom-call(bf16[512,512]{1,0:T(8,128)(2,1)S(1)} %get-tuple-element., ...), custom_call_target="tpu_custom_call" | custom-call | flops 1610612736 | bytes 4194304 | tf_op jit(solution)/shard_map/pallas_call | solution.py:94
  14.6 0.0 collective-permute-done.2.refs_1_
  14.6 0.9 %collective-permute-start.9 = (f32[448,128]{1,0:T(8,128)S(1)}, f32[448,128]{1,0:T(8,128)S(1)}, u32[]{:S(2)}, u32[]{:S(2)}) collective-permute-start(f32[448,128]{1,0:T(8,128)S(1)} %get-tuple-element.39), channel_id=1, source_target_pairs={{2,0},{3,1},{4,6},{5,7},{0,2},{1,3},{6,4},{7,5},{10,8},{11,9},{12,... | collective-permute-start | bytes 688136 | tf_op jit(solution)/shard_map/ppermute | solution.py:319
  15.5 0.0 collective-permute-done.3.refs_2_
  15.5 0.0 copy-done.2
  15.5 2.4 %collective-permute-start.4 = (f32[256,256]{1,0:T(8,128)S(1)}, f32[256,256]{1,0:T(8,128)S(1)}, u32[]{:S(2)}, u32[]{:S(2)}) collective-permute-start(f32[256,256]{1,0:T(8,128)S(1)} %copy-done.2), channel_id=1, source_target_pairs={{0,24},{8,16},{16,8},{24,0},{1,25},{9,17},{17,9},{25,1},{2,26},{10... | collective-permute-start | bytes 786440 | tf_op jit(solution)/shard_map/ppermute | solution.py:325
  18.0 0.0 collective-permute-done.8.refs_6_.middle
  18.0 0.0 copy-done.1
  18.0 0.0 collective-permute-start.5
  18.0 5.0 %collective-permute-done.6.refs_4_ = f32[512,128]{1,0:T(8,128)S(1)} collective-permute-done((f32[512,128]{1,0:T(8,128)}, f32[512,128]{1,0:T(8,128)S(1)}, u32[]{:S(2)}, u32[]{:S(2)}) %collective-permute-start.6) | collective-permute-done | bytes 262176 | tf_op jit(solution)/shard_map/ppermute | solution.py:319
  23.0 0.0 collective-permute-start.7
  23.0 4.8 %collective-permute-done.9.refs_7_ = f32[448,128]{1,0:T(8,128)S(1)} collective-permute-done((f32[448,128]{1,0:T(8,128)S(1)}, f32[448,128]{1,0:T(8,128)S(1)}, u32[]{:S(2)}, u32[]{:S(2)}) %collective-permute-start.9) | collective-permute-done | bytes 229408 | tf_op jit(solution)/shard_map/ppermute | solution.py:319
  27.8 0.1 collective-permute-start.10
  27.9 0.0 collective-permute-done.1.other.refs_3_
  27.9 0.4 %collective-permute-start.11 = (f32[448,128]{1,0:T(8,128)S(1)}, f32[448,128]{1,0:T(8,128)S(1)}, u32[]{:S(2)}, u32[]{:S(2)}) collective-permute-start(f32[448,128]{1,0:T(8,128)S(1)} %collective-permute-done.9.refs_7_), channel_id=1, source_target_pairs={{0,1},{1,0},{2,3},{3,2},{4,5},{5,4},{6,7},{7,6},{8,9},{9,8},{10,11... | collective-permute-start | bytes 688136 | tf_op jit(solution)/shard_map/ppermute | solution.py:319
  28.3 2.0 %shard_map.48 = (bf16[512,512]{1,0:T(8,128)(2,1)S(1)}, bf16[512,512]{1,0:T(8,128)(2,1)S(1)}, f32[128,128]{1,0:T(8,128)S(1)}) custom-call(f32[512,512]{1,0:T(8,128)S(1)} %get-tuple-element.32.e, bf16[512,512]{1,0:T(8,128)(2,1)S(1)} %get-tuple-element.33.eh, bf16[512,512]{1,0:T(8,128)(2,1)S(1)} %get-tuple-element.34.el, ...), custom_call_target="tpu_custom_call" | custom-call | flops 1610612736 | bytes 4194304 | tf_op jit(solution)/shard_map/pallas_call | solution.py:94
  30.3 0.0 copy-start
  30.3 0.0 collective-permute-done.4.refs_3_
  30.3 0.1 collective-permute-start.12
  30.4 2.5 %chain_part.1 = (bf16[1024,256]{1,0:T(8,128)(2,1)S(1)}, bf16[1024,256]{1,0:T(8,128)(2,1)S(1)}) custom-call(bf16[512,512]{1,0:T(8,128)(2,1)S(1)} %get-tuple-element.23.g1h, bf16[512,512]{1,0:T(8,128)(2,1)S(1)} %get-tuple-element.24.g1l, bf16[512,512]{1,0:T(8,128)(2,1)S(1)} %get-tuple-element.28.vh, bf16[512,512]{1,0:T(8,128)(2,1)S(1)} %get-tuple-element.29.vl, ...), custom_call_target="tpu_custom_call" | custom-call | flops 1610612736 | bytes 6291456 | tf_op jit(solution)/shard_map/chain_part/pallas_call | solution.py:202
  32.9 0.0 collective-permute-done.5.refs_1_
  32.9 0.0 collective-permute-done.7.refs_5_
  32.9 0.0 copy-done
  32.9 1.0 %update_part.1.part = f32[512,256]{1,0:T(8,128)S(1)} custom-call(f32[512,256]{1,0:T(8,128)S(1)} %copy-done, bf16[1024,256]{1,0:T(8,128)(2,1)S(1)} %get-tuple-element.37.yh, bf16[1024,256]{1,0:T(8,128)(2,1)S(1)} %get-tuple-element.38.yl, f32[512,128]{1,0:T(8,128)S(1)} %copy-done.1, f32[512,128]{1,0:T(8,128)S(1)} %collective-permute-done.5.refs_1_, ...), custom_call_target="tpu_custom_call" | custom-call | flops 805306368 | bytes 3145728 | tf_op jit(solution)/shard_map/update_part/pallas_call | solution.py:266
  33.9 0.0 collective-permute-done.10.middle_other
  33.9 0.7 %collective-permute-done.12.tails = f32[128,128]{1,0:T(8,128)S(1)} collective-permute-done((f32[128,128]{1,0:T(8,128)S(1)}, f32[128,128]{1,0:T(8,128)S(1)}, u32[]{:S(2)}, u32[]{:S(2)}) %collective-permute-start.12) | collective-permute-done | bytes 65568 | tf_op jit(solution)/shard_map/ppermute | solution.py:319
  34.6 0.0 collective-permute-done.11.head_other
  34.6 1.1 %last_part.1 = f32[512,256]{1,0:T(8,128)} custom-call(f32[512,256]{1,0:T(8,128)S(1)} %update_part.1.part, bf16[1024,256]{1,0:T(8,128)(2,1)S(1)} %get-tuple-element.37.yh, bf16[1024,256]{1,0:T(8,128)(2,1)S(1)} %get-tuple-element.38.yl, f32[512,128]{1,0:T(8,128)S(1)} %collective-permute-done.8.refs_6_.middle, ...), custom_call_target="tpu_custom_call" | custom-call | flops 100663296 | bytes 1572864 | tf_op jit(solution)/shard_map/last_part/pallas_call | solution.py:300
Async XLA Ops:
  0.0 12.5 %collective-permute-start = (f32[512,128]{1,0:T(8,128)}, f32[512,128]{1,0:T(8,128)S(1)}, u32[]{:S(2)}, u32[]{:S(2)}) collective-permute-start(f32[512,128]{1,0:T(8,128)} %refs_0_.3), channel_id=1, source_target_pairs={{2,0},{3,1},{6,2},{7,3},{0,4},{1,5},{4,6},{5,7},{10,8},{11,9},{14,... | collective-permute-start | bytes 786440 | tf_op jit(solution)/shard_map/ppermute | solution.py:319
  4.1 10.5 %collective-permute-start.2 = (f32[256,256]{1,0:T(8,128)}, f32[256,256]{1,0:T(8,128)S(1)}, u32[]{:S(2)}, u32[]{:S(2)}) collective-permute-start(f32[256,256]{1,0:T(8,128)} %refs_0_.2), channel_id=1, source_target_pairs={{0,8},{8,0},{16,24},{24,16},{1,9},{9,1},{17,25},{25,17},{2,10},{10... | collective-permute-start | bytes 786440 | tf_op jit(solution)/shard_map/ppermute | solution.py:325
  5.6 10.0 %collective-permute-start.3 = (f32[256,256]{1,0:T(8,128)}, f32[256,256]{1,0:T(8,128)S(1)}, u32[]{:S(2)}, u32[]{:S(2)}) collective-permute-start(f32[256,256]{1,0:T(8,128)} %refs_0_.2), channel_id=1, source_target_pairs={{0,16},{8,24},{16,0},{24,8},{1,17},{9,25},{17,1},{25,9},{2,18},{10... | collective-permute-start | bytes 786440 | tf_op jit(solution)/shard_map/ppermute | solution.py:325
  7.1 10.9 %collective-permute-start.8 = (f32[512,128]{1,0:T(8,128)}, f32[512,128]{1,0:T(8,128)S(1)}, u32[]{:S(2)}, u32[]{:S(2)}) collective-permute-start(f32[512,128]{1,0:T(8,128)} %refs_0_.3), channel_id=1, source_target_pairs={{2,4},{3,5},{4,2},{5,3},{0,1},{1,0},{6,7},{7,6},{10,12},{11,13},{1... | collective-permute-start | bytes 786440 | tf_op jit(solution)/shard_map/ppermute | solution.py:319
  7.1 15.9 %collective-permute-start.6 = (f32[512,128]{1,0:T(8,128)}, f32[512,128]{1,0:T(8,128)S(1)}, u32[]{:S(2)}, u32[]{:S(2)}) collective-permute-start(f32[512,128]{1,0:T(8,128)} %refs_0_.3), channel_id=1, source_target_pairs={{4,0},{5,1},{0,2},{1,3},{6,4},{7,5},{2,6},{3,7},{12,8},{13,9},{8,1... | collective-permute-start | bytes 786440 | tf_op jit(solution)/shard_map/ppermute | solution.py:319
  12.4 3.1 %copy-start.2 = (f32[256,256]{1,0:T(8,128)S(1)}, f32[256,256]{1,0:T(8,128)}, u32[]{:S(2)}) copy-start(f32[256,256]{1,0:T(8,128)} %refs_0_.2) | copy-start | bytes 786436
  12.5 5.5 %copy-start.1 = (f32[512,128]{1,0:T(8,128)S(1)}, f32[512,128]{1,0:T(8,128)}, u32[]{:S(2)}) copy-start(f32[512,128]{1,0:T(8,128)} %refs_0_.3) | copy-start | bytes 786436
  12.5 15.4 %collective-permute-start.1 = (f32[512,128]{1,0:T(8,128)S(1)}, f32[512,128]{1,0:T(8,128)S(1)}, u32[]{:S(2)}, u32[]{:S(2)}) collective-permute-start(f32[512,128]{1,0:T(8,128)S(1)} %collective-permute-done.shard.own.refs_2_), channel_id=1, source_target_pairs={{0,1},{1,0},{2,3},{3,2},{4,5},{5,4},{6,7},{7,6},{8,9},{9,8},{10,11... | collective-permute-start | bytes 786440 | tf_op jit(solution)/shard_map/ppermute | solution.py:319
  14.6 13.2 %collective-permute-start.9 = (f32[448,128]{1,0:T(8,128)S(1)}, f32[448,128]{1,0:T(8,128)S(1)}, u32[]{:S(2)}, u32[]{:S(2)}) collective-permute-start(f32[448,128]{1,0:T(8,128)S(1)} %get-tuple-element.39), channel_id=1, source_target_pairs={{2,0},{3,1},{4,6},{5,7},{0,2},{1,3},{6,4},{7,5},{10,8},{11,9},{12,... | collective-permute-start | bytes 688136 | tf_op jit(solution)/shard_map/ppermute | solution.py:319
  15.5 14.8 %collective-permute-start.4 = (f32[256,256]{1,0:T(8,128)S(1)}, f32[256,256]{1,0:T(8,128)S(1)}, u32[]{:S(2)}, u32[]{:S(2)}) collective-permute-start(f32[256,256]{1,0:T(8,128)S(1)} %copy-done.2), channel_id=1, source_target_pairs={{0,24},{8,16},{16,8},{24,0},{1,25},{9,17},{17,9},{25,1},{2,26},{10... | collective-permute-start | bytes 786440 | tf_op jit(solution)/shard_map/ppermute | solution.py:325
  18.0 14.9 %collective-permute-start.5 = (f32[512,128]{1,0:T(8,128)S(1)}, f32[512,128]{1,0:T(8,128)S(1)}, u32[]{:S(2)}, u32[]{:S(2)}) collective-permute-start(f32[512,128]{1,0:T(8,128)S(1)} %copy-done.1), channel_id=1, source_target_pairs={{0,1},{1,0},{2,3},{3,2},{4,5},{5,4},{6,7},{7,6},{8,9},{9,8},{10,11... | collective-permute-start | bytes 786440 | tf_op jit(solution)/shard_map/ppermute | solution.py:319
  23.0 9.9 %collective-permute-start.7 = (f32[512,128]{1,0:T(8,128)S(1)}, f32[512,128]{1,0:T(8,128)S(1)}, u32[]{:S(2)}, u32[]{:S(2)}) collective-permute-start(f32[512,128]{1,0:T(8,128)S(1)} %collective-permute-done.6.refs_4_), channel_id=1, source_target_pairs={{0,1},{1,0},{2,3},{3,2},{4,5},{5,4},{6,7},{7,6},{8,9},{9,8},{10,11... | collective-permute-start | bytes 786440 | tf_op jit(solution)/shard_map/ppermute | solution.py:319
  27.8 6.1 %collective-permute-start.10 = (f32[512,128]{1,0:T(8,128)S(1)}, f32[512,128]{1,0:T(8,128)S(1)}, u32[]{:S(2)}, u32[]{:S(2)}) collective-permute-start(f32[512,128]{1,0:T(8,128)S(1)} %collective-permute-done.8.refs_6_.middle), channel_id=1, source_target_pairs={{0,1},{1,0},{2,3},{3,2},{4,5},{5,4},{6,7},{7,6},{8,9},{9,8},{10,11... | collective-permute-start | bytes 786440 | tf_op jit(solution)/shard_map/ppermute | solution.py:319
  27.9 6.8 %collective-permute-start.11 = (f32[448,128]{1,0:T(8,128)S(1)}, f32[448,128]{1,0:T(8,128)S(1)}, u32[]{:S(2)}, u32[]{:S(2)}) collective-permute-start(f32[448,128]{1,0:T(8,128)S(1)} %collective-permute-done.9.refs_7_), channel_id=1, source_target_pairs={{0,1},{1,0},{2,3},{3,2},{4,5},{5,4},{6,7},{7,6},{8,9},{9,8},{10,11... | collective-permute-start | bytes 688136 | tf_op jit(solution)/shard_map/ppermute | solution.py:319
  30.3 2.7 %copy-start = (f32[512,256]{1,0:T(8,128)S(1)}, f32[512,256]{1,0:T(8,128)}, u32[]{:S(2)}) copy-start(f32[512,256]{1,0:T(8,128)} %trail.1) | copy-start | bytes 1572868
  30.3 4.3 %collective-permute-start.12 = (f32[128,128]{1,0:T(8,128)S(1)}, f32[128,128]{1,0:T(8,128)S(1)}, u32[]{:S(2)}, u32[]{:S(2)}) collective-permute-start(f32[128,128]{1,0:T(8,128)S(1)} %get-tuple-element.40), channel_id=1, source_target_pairs={{2,0},{3,1},{4,6},{5,7},{0,2},{1,3},{6,4},{7,5},{10,8},{11,9},{12,... | collective-permute-start | bytes 196616 | tf_op jit(solution)/shard_map/ppermute | solution.py:319

commit v5 on v4

--- a/solution.py
+++ b/solution.py
@@ -39,9 +39,9 @@
     return jnp.where(row == col + first, 1.0, 0.0).astype(F32)
 
 
-def each(n, body):
+def each(n, body, skip=0, stop=None):
     step = min(256, n)
-    for first in range(0, n, step):
+    for first in list(range(0, n, step))[skip:stop]:
         body(pl.ds(first, step), first)
 
 
@@ -53,13 +53,16 @@
     return dot3((left[0][...], left[1][...]), (right[0][:, cols], right[1][:, cols]))
 
 
-def powers(n, x, e, f, g):
+def squares(n, x, e, f, **part):
     def square(cols, _):
-        s = product(e, e, cols)
-        put(f, cols, s)
-        x[:, cols] = x[:, cols] + s
-
-    each(n, square)
+        y = product(e, e, cols)
+        put(f, cols, y)
+        x[:, cols] = x[:, cols] + y
+
+    each(n, square, **part)
+
+
+def cubes(n, x, e, f, g):
     each(n, lambda cols, _: put(g, cols, x[:, cols] + product(e, f, cols)))
 
 
@@ -83,12 +86,13 @@
         put((eh, el), cols, x)
 
     each(n, residual)
-    powers(n, a, (eh, el), (fh, fl), (g1h, g1l))
+    squares(n, a, (eh, el), (fh, fl))
+    cubes(n, a, (eh, el), (fh, fl), (g1h, g1l))
     for copy in copies[1:]:
         copy.wait()
 
 
-def kernel_call(body, name, outs, ins, scratch, products, limit=16):
+def kernel_call(body, name, outs, ins, scratch, products, limit=16, aliases={}):
     n = outs[0].shape[0]
     specs = [pl.BlockSpec(memory_space=pltpu.HBM if name == "first_part" else pltpu.VMEM)] * len(ins)
     return pl.pallas_call(
@@ -97,6 +101,7 @@
         in_specs=specs,
         out_specs=(VMEM,) * len(outs),
         scratch_shapes=scratch,
+        input_output_aliases=aliases,
         cost_estimate=pl.CostEstimate(flops=int(6 * products * n * n * n), bytes_accessed=16 * n * n, transcendentals=0),
         compiler_params=pltpu.CompilerParams(vmem_limit_bytes=limit << 20),
     )(*ins)
@@ -141,19 +146,43 @@
     return kernel_call(second_kernel, "second_part", outs, (*g1, u, l, d, shard), [pltpu.VMEM((n, n), BF16)] * 2, 2)
 
 
-def third_kernel(e, eh, el, own, other, g2h, g2l, tails, x, fh, fl):
+def third_kernel(e, eh, el, own, other, g2h, g2l, x, fh, fl, tails):
     n = e.shape[0]
     for i, shard in enumerate((own, other)):
         tails[pl.ds(i * TAIL, TAIL), :] = shard[pl.ds(shard.shape[0] - TAIL, TAIL), :]
-    x[...] = e[...]
-    powers(n, x, (eh, el), (fh, fl), (g2h, g2l))
+
+    @pl.when(at_end())
+    def _():
+        x[...] = e[...]
+        squares(n, x, (eh, el), (fh, fl))
+        cubes(n, x, (eh, el), (fh, fl), (g2h, g2l))
+
+    @pl.when(jnp.logical_not(at_end()))
+    def _():
+        x[...] = e[...]
+        squares(n, x, (eh, el), (fh, fl), stop=1)
 
 
 def third_part(e, own, other):
     n = e[0].shape[0]
-    outs = [half(n, n)] * 2 + [single(2 * TAIL, own.shape[1])]
-    scratch = [pltpu.VMEM((n, n), F32)] + [pltpu.VMEM((n, n), BF16)] * 2
-    return kernel_call(third_kernel, "third_part", outs, (*e, own, other), scratch, 2)
+    outs = [half(n, n)] * 2 + [single(n, n)] + [half(n, n)] * 2 + [single(2 * TAIL, own.shape[1])]
+    return kernel_call(third_kernel, "third_part", outs, (*e, own, other), [], 2)
+
+
+def late_kernel(eh, el, *refs):
+    g2h, g2l, x, fh, fl = refs[-5:]
+
+    @pl.when(jnp.logical_not(at_end()))
+    def _():
+        n = eh.shape[0]
+        squares(n, x, (eh, el), (fh, fl), skip=1)
+        cubes(n, x, (eh, el), (fh, fl), (g2h, g2l))
+
+
+def late_part(e, work):
+    n = e[0].shape[0]
+    outs = [half(n, n)] * 2 + [single(n, n)] + [half(n, n)] * 2
+    return kernel_call(late_kernel, "late_part", outs, (*e[1:], *work), [], 2, aliases={2 + i: i for i in range(5)})
 
 
 def chain_kernel(g1h, g1l, vh, vl, lowh, lowl, g2h, g2l, *refs):
@@ -332,8 +361,9 @@
     *g1, u, l, d = first_part(pivot)
     vh, vl, lowh, lowl, *e, head = second_part(g1, u, l, d, one)
     head = send(head, SEND_ENDS)
-    *g2, tails = third_part(e, one, one_other)
+    *work, tails = third_part(e, one, one_other)
     tails = send(tails, SEND_ENDS)
+    g2 = late_part(e, work)[:2]
     y = chain_part(g1, (vh, vl), (lowh, lowl), g2, rows)
     pieces = [col_panel, exchange(col_panel), one, one_other, two, exchange(two)]
     part = update_part((chips, HOP_ONE, HOP_TWO), trailing, y, pieces + [middle, head])

time: 35.9 us -> 33.8 us (0.942)
  waiting for transfers between devices: 10.5 us -> 6.03 us
  starting transfers between devices: 13.2 us -> 15.6 us
    ppermute x10, waiting for transfers between devices: 10.5 us -> 5.82 us  [send(): return lax.ppermute(x, 'col', hops + swaps)]
    ppermute x10, starting transfers between devices: 7.75 us -> 10.2 us  [send(): return lax.ppermute(x, 'col', hops + swaps)]
    pallas_call x3 -> x4, Pallas kernels: 7.22 us -> 7.21 us  [kernel_call(): pl.pallas_call(body, out_shape=tuple(outs), in_specs=specs, out_specs=(VM...]
  transfers between devices with their start and end apart: 13 -> 13, of which waited for: 3 -> 3; matrix products, arithmetic and copies ran while one was open for 0% -> 0% of each run, Pallas kernels for 30% -> 32%
where the time goes in v5:
time: 33.8 us; the launch traced here: 33.7 us
  starting transfers between devices  15.6 us (46%)
  Pallas kernels  11.8 us (35%)
  waiting for transfers between devices  6.03 us (18%)
    ppermute x10, starting transfers between devices, send(): return lax.ppermute(x, 'col', hops + swaps)  10.2 us
    pallas_call x4, Pallas kernels, kernel_call(): pl.pallas_call(body, out_shape=tuple(outs), in_specs=specs, out_specs=(VM...  7.21 us
    ppermute x10, waiting for transfers between devices, send(): return lax.ppermute(x, 'col', hops + swaps)  5.82 us
    ppermute x3, starting transfers between devices, row(): return lax.ppermute(row_panel, 'row', [(i, i ^ s) for i in range(n_row)])  5.47 us
    pallas_call x1, Pallas kernels, chain_part(): pl.pallas_call(chain_kernel, out_shape=(half(2 * n, width),) * 2, in_spec...  2.52 us
    pallas_call x1, Pallas kernels, last_part(): pl.pallas_call(functools.partial(last_kernel, blocks), out_shape=jax.Shap...  1.12 us
    pallas_call x1, Pallas kernels, update_part(): pl.pallas_call(functools.partial(update_kernel, tables), out_shape=jax.Sh...  0.98 us
  transfers between devices with their start and end apart: 13, of which 3 were waited for; matrix products, arithmetic and copies ran while one was open for 0% of the time, Pallas kernels for 32%

profile of v5, /device:TPU:0, one launch (start us, length us, event | category | flops | bytes accessed | tf_op | source)
XLA Modules:
  0.0 33.7 jit_solution(10782300917049418203)
XLA Ops:
  0.0 4.1 %collective-permute-start = (f32[512,128]{1,0:T(8,128)}, f32[512,128]{1,0:T(8,128)S(1)}, u32[]{:S(2)}, u32[]{:S(2)}) collective-permute-start(f32[512,128]{1,0:T(8,128)} %refs_0_.3), channel_id=1, source_target_pairs={{2,0},{3,1},{6,2},{7,3},{0,4},{1,5},{4,6},{5,7},{10,8},{11,9},{14,... | collective-permute-start | bytes 786440 | tf_op jit(solution)/shard_map/ppermute | solution.py:348
  4.1 1.5 %collective-permute-start.2 = (f32[256,256]{1,0:T(8,128)}, f32[256,256]{1,0:T(8,128)S(1)}, u32[]{:S(2)}, u32[]{:S(2)}) collective-permute-start(f32[256,256]{1,0:T(8,128)} %refs_0_.2), channel_id=1, source_target_pairs={{0,8},{8,0},{16,24},{24,16},{1,9},{9,1},{17,25},{25,17},{2,10},{10... | collective-permute-start | bytes 786440 | tf_op jit(solution)/shard_map/ppermute | solution.py:354
  5.6 1.5 %collective-permute-start.3 = (f32[256,256]{1,0:T(8,128)}, f32[256,256]{1,0:T(8,128)S(1)}, u32[]{:S(2)}, u32[]{:S(2)}) collective-permute-start(f32[256,256]{1,0:T(8,128)} %refs_0_.2), channel_id=1, source_target_pairs={{0,16},{8,24},{16,0},{24,8},{1,17},{9,25},{17,1},{25,9},{2,18},{10... | collective-permute-start | bytes 786440 | tf_op jit(solution)/shard_map/ppermute | solution.py:354
  7.1 0.0 collective-permute-start.8
  7.1 2.1 %collective-permute-start.6 = (f32[512,128]{1,0:T(8,128)}, f32[512,128]{1,0:T(8,128)S(1)}, u32[]{:S(2)}, u32[]{:S(2)}) collective-permute-start(f32[512,128]{1,0:T(8,128)} %refs_0_.3), channel_id=1, source_target_pairs={{4,0},{5,1},{0,2},{1,3},{6,4},{7,5},{2,6},{3,7},{12,8},{13,9},{8,1... | collective-permute-start | bytes 786440 | tf_op jit(solution)/shard_map/ppermute | solution.py:348
  9.2 1.9 %collective-permute-done.shard.own.refs_2_ = f32[512,128]{1,0:T(8,128)S(1)} collective-permute-done((f32[512,128]{1,0:T(8,128)}, f32[512,128]{1,0:T(8,128)S(1)}, u32[]{:S(2)}, u32[]{:S(2)}) %collective-permute-start) | collective-permute-done | bytes 262176 | tf_op jit(solution)/shard_map/ppermute | solution.py:348
  11.1 0.0 collective-permute-start.1
  11.1 3.2 %shard_map.46 = (bf16[512,512]{1,0:T(8,128)(2,1)S(1)}, bf16[512,512]{1,0:T(8,128)(2,1)S(1)}, f32[512,512]{1,0:T(8,128)S(1)}, f32[512,512]{1,0:T(8,128)S(1)}, f32[512,512]{1,0:T(8,128)S(1)}) custom-call(f32[1024,1024]{1,0:T(8,128)} %pivot.1), custom_call_target="tpu_custom_call" | custom-call | flops 1610612736 | bytes 4194304 | tf_op jit(solution)/shard_map/pallas_call | solution.py:98
  14.3 0.0 copy-start.2
  14.3 2.0 %shard_map.47 = (bf16[512,512]{1,0:T(8,128)(2,1)S(1)}, bf16[512,512]{1,0:T(8,128)(2,1)S(1)}, bf16[512,512]{1,0:T(8,128)(2,1)S(1)}, bf16[512,512]{1,0:T(8,128)(2,...) custom-call(bf16[512,512]{1,0:T(8,128)(2,1)S(1)} %get-tuple-element., ...), custom_call_target="tpu_custom_call" | custom-call | flops 1610612736 | bytes 4194304 | tf_op jit(solution)/shard_map/pallas_call | solution.py:98
  16.4 0.0 copy-start.1
  16.4 0.0 collective-permute-done.2.refs_1_
  16.4 2.4 %collective-permute-start.9 = (f32[448,128]{1,0:T(8,128)S(1)}, f32[448,128]{1,0:T(8,128)S(1)}, u32[]{:S(2)}, u32[]{:S(2)}) collective-permute-start(f32[448,128]{1,0:T(8,128)S(1)} %get-tuple-element.49), channel_id=1, source_target_pairs={{2,0},{3,1},{4,6},{5,7},{0,2},{1,3},{6,4},{7,5},{10,8},{11,9},{12,... | collective-permute-start | bytes 688136 | tf_op jit(solution)/shard_map/ppermute | solution.py:348
  18.8 0.0 collective-permute-done.1.other.refs_3_
  18.8 0.0 copy-done.2
  18.8 2.5 %collective-permute-start.4 = (f32[256,256]{1,0:T(8,128)S(1)}, f32[256,256]{1,0:T(8,128)S(1)}, u32[]{:S(2)}, u32[]{:S(2)}) collective-permute-start(f32[256,256]{1,0:T(8,128)S(1)} %copy-done.2), channel_id=1, source_target_pairs={{0,24},{8,16},{16,8},{24,0},{1,25},{9,17},{17,9},{25,1},{2,26},{10... | collective-permute-start | bytes 786440 | tf_op jit(solution)/shard_map/ppermute | solution.py:354
  21.2 1.9 %shard_map.48 = (bf16[512,512]{1,0:T(8,128)(2,1)S(1)}, bf16[512,512]{1,0:T(8,128)(2,1)S(1)}, f32[512,512]{1,0:T(8,128)S(1)}, bf16[512,512]{1,0:T(8,128)(2,1)S(1)...) custom-call(f32[512,512]{1,0:T(8,128)S(1)} %get-tuple-element.39.e, bf16[512,512]{1,0:T(8,128)(2,1)S(1)} %get-tuple-element.37.eh, ...), custom_call_target="tpu_custom_call" | custom-call | flops 1610612736 | bytes 4194304 | tf_op jit(solution)/shard_map/pallas_call | solution.py:98
  23.2 0.0 collective-permute-done.3.refs_2_
  23.2 0.0 copy-done.1
  23.2 0.1 collective-permute-start.5
  23.3 0.0 collective-permute-done.6.refs_4_
  23.3 0.5 %collective-permute-start.7 = (f32[512,128]{1,0:T(8,128)S(1)}, f32[512,128]{1,0:T(8,128)S(1)}, u32[]{:S(2)}, u32[]{:S(2)}) collective-permute-start(f32[512,128]{1,0:T(8,128)S(1)} %collective-permute-done.6.refs_4_), channel_id=1, source_target_pairs={{0,1},{1,0},{2,3},{3,2},{4,5},{5,4},{6,7},{7,6},{8,9},{9,8},{10,11... | collective-permute-start | bytes 786440 | tf_op jit(solution)/shard_map/ppermute | solution.py:348
  23.8 0.0 collective-permute-done.8.refs_6_.middle
  23.8 0.1 collective-permute-start.10
  23.9 3.9 %collective-permute-done.9.refs_7_ = f32[448,128]{1,0:T(8,128)S(1)} collective-permute-done((f32[448,128]{1,0:T(8,128)S(1)}, f32[448,128]{1,0:T(8,128)S(1)}, u32[]{:S(2)}, u32[]{:S(2)}) %collective-permute-start.9) | collective-permute-done | bytes 229408 | tf_op jit(solution)/shard_map/ppermute | solution.py:348
  27.8 0.1 collective-permute-start.11
  27.9 0.0 copy-start
  27.9 0.2 collective-permute-done.4.refs_3_
  28.1 0.9 %collective-permute-start.12 = (f32[128,128]{1,0:T(8,128)S(1)}, f32[128,128]{1,0:T(8,128)S(1)}, u32[]{:S(2)}, u32[]{:S(2)}) collective-permute-start(f32[128,128]{1,0:T(8,128)S(1)} %get-tuple-element.50), channel_id=1, source_target_pairs={{2,0},{3,1},{4,6},{5,7},{0,2},{1,3},{6,4},{7,5},{10,8},{11,9},{12,... | collective-permute-start | bytes 196616 | tf_op jit(solution)/shard_map/ppermute | solution.py:348
  29.0 2.5 %chain_part.1 = (bf16[1024,256]{1,0:T(8,128)(2,1)S(1)}, bf16[1024,256]{1,0:T(8,128)(2,1)S(1)}) custom-call(bf16[512,512]{1,0:T(8,128)(2,1)S(1)} %get-tuple-element.28.g1h, bf16[512,512]{1,0:T(8,128)(2,1)S(1)} %get-tuple-element.29.g1l, bf16[512,512]{1,0:T(8,128)(2,1)S(1)} %get-tuple-element.33.vh, bf16[512,512]{1,0:T(8,128)(2,1)S(1)} %get-tuple-element.34.vl, ...), custom_call_target="tpu_custom_call" | custom-call | flops 1610612736 | bytes 6291456 | tf_op jit(solution)/shard_map/chain_part/pallas_call | solution.py:231
  31.5 0.0 collective-permute-done.5.refs_1_
  31.5 0.0 collective-permute-done.7.refs_5_
  31.5 0.0 copy-done
  31.5 1.0 %update_part.1.part = f32[512,256]{1,0:T(8,128)S(1)} custom-call(f32[512,256]{1,0:T(8,128)S(1)} %copy-done, bf16[1024,256]{1,0:T(8,128)(2,1)S(1)} %get-tuple-element.47.yh, bf16[1024,256]{1,0:T(8,128)(2,1)S(1)} %get-tuple-element.48.yl, f32[512,128]{1,0:T(8,128)S(1)} %copy-done.1, f32[512,128]{1,0:T(8,128)S(1)} %collective-permute-done.5.refs_1_, ...), custom_call_target="tpu_custom_call" | custom-call | flops 805306368 | bytes 3145728 | tf_op jit(solution)/shard_map/update_part/pallas_call | solution.py:295
  32.5 0.0 collective-permute-done.10.middle_other
  32.5 0.0 collective-permute-done.12.tails
  32.5 0.0 collective-permute-done.11.head_other
  32.6 1.1 %last_part.1 = f32[512,256]{1,0:T(8,128)} custom-call(f32[512,256]{1,0:T(8,128)S(1)} %update_part.1.part, bf16[1024,256]{1,0:T(8,128)(2,1)S(1)} %get-tuple-element.47.yh, bf16[1024,256]{1,0:T(8,128)(2,1)S(1)} %get-tuple-element.48.yl, f32[512,128]{1,0:T(8,128)S(1)} %collective-permute-done.8.refs_6_.middle, ...), custom_call_target="tpu_custom_call" | custom-call | flops 100663296 | bytes 1572864 | tf_op jit(solution)/shard_map/last_part/pallas_call | solution.py:329
  (1 shorter events, 0.0 us)
Async XLA Ops:
  0.0 11.1 %collective-permute-start = (f32[512,128]{1,0:T(8,128)}, f32[512,128]{1,0:T(8,128)S(1)}, u32[]{:S(2)}, u32[]{:S(2)}) collective-permute-start(f32[512,128]{1,0:T(8,128)} %refs_0_.3), channel_id=1, source_target_pairs={{2,0},{3,1},{6,2},{7,3},{0,4},{1,5},{4,6},{5,7},{10,8},{11,9},{14,... | collective-permute-start | bytes 786440 | tf_op jit(solution)/shard_map/ppermute | solution.py:348
  4.1 12.3 %collective-permute-start.2 = (f32[256,256]{1,0:T(8,128)}, f32[256,256]{1,0:T(8,128)S(1)}, u32[]{:S(2)}, u32[]{:S(2)}) collective-permute-start(f32[256,256]{1,0:T(8,128)} %refs_0_.2), channel_id=1, source_target_pairs={{0,8},{8,0},{16,24},{24,16},{1,9},{9,1},{17,25},{25,17},{2,10},{10... | collective-permute-start | bytes 786440 | tf_op jit(solution)/shard_map/ppermute | solution.py:354
  5.6 17.6 %collective-permute-start.3 = (f32[256,256]{1,0:T(8,128)}, f32[256,256]{1,0:T(8,128)S(1)}, u32[]{:S(2)}, u32[]{:S(2)}) collective-permute-start(f32[256,256]{1,0:T(8,128)} %refs_0_.2), channel_id=1, source_target_pairs={{0,16},{8,24},{16,0},{24,8},{1,17},{9,25},{17,1},{25,9},{2,18},{10... | collective-permute-start | bytes 786440 | tf_op jit(solution)/shard_map/ppermute | solution.py:354
  7.1 16.7 %collective-permute-start.8 = (f32[512,128]{1,0:T(8,128)}, f32[512,128]{1,0:T(8,128)S(1)}, u32[]{:S(2)}, u32[]{:S(2)}) collective-permute-start(f32[512,128]{1,0:T(8,128)} %refs_0_.3), channel_id=1, source_target_pairs={{2,4},{3,5},{4,2},{5,3},{0,1},{1,0},{6,7},{7,6},{10,12},{11,13},{1... | collective-permute-start | bytes 786440 | tf_op jit(solution)/shard_map/ppermute | solution.py:348
  7.1 16.2 %collective-permute-start.6 = (f32[512,128]{1,0:T(8,128)}, f32[512,128]{1,0:T(8,128)S(1)}, u32[]{:S(2)}, u32[]{:S(2)}) collective-permute-start(f32[512,128]{1,0:T(8,128)} %refs_0_.3), channel_id=1, source_target_pairs={{4,0},{5,1},{0,2},{1,3},{6,4},{7,5},{2,6},{3,7},{12,8},{13,9},{8,1... | collective-permute-start | bytes 786440 | tf_op jit(solution)/shard_map/ppermute | solution.py:348
  11.1 7.7 %collective-permute-start.1 = (f32[512,128]{1,0:T(8,128)S(1)}, f32[512,128]{1,0:T(8,128)S(1)}, u32[]{:S(2)}, u32[]{:S(2)}) collective-permute-start(f32[512,128]{1,0:T(8,128)S(1)} %collective-permute-done.shard.own.refs_2_), channel_id=1, source_target_pairs={{0,1},{1,0},{2,3},{3,2},{4,5},{5,4},{6,7},{7,6},{8,9},{9,8},{10,11... | collective-permute-start | bytes 786440 | tf_op jit(solution)/shard_map/ppermute | solution.py:348
  14.3 4.4 %copy-start.2 = (f32[256,256]{1,0:T(8,128)S(1)}, f32[256,256]{1,0:T(8,128)}, u32[]{:S(2)}) copy-start(f32[256,256]{1,0:T(8,128)} %refs_0_.2) | copy-start | bytes 786436
  16.4 6.8 %copy-start.1 = (f32[512,128]{1,0:T(8,128)S(1)}, f32[512,128]{1,0:T(8,128)}, u32[]{:S(2)}) copy-start(f32[512,128]{1,0:T(8,128)} %refs_0_.3) | copy-start | bytes 786436
  16.4 11.4 %collective-permute-start.9 = (f32[448,128]{1,0:T(8,128)S(1)}, f32[448,128]{1,0:T(8,128)S(1)}, u32[]{:S(2)}, u32[]{:S(2)}) collective-permute-start(f32[448,128]{1,0:T(8,128)S(1)} %get-tuple-element.49), channel_id=1, source_target_pairs={{2,0},{3,1},{4,6},{5,7},{0,2},{1,3},{6,4},{7,5},{10,8},{11,9},{12,... | collective-permute-start | bytes 688136 | tf_op jit(solution)/shard_map/ppermute | solution.py:348
  18.8 9.3 %collective-permute-start.4 = (f32[256,256]{1,0:T(8,128)S(1)}, f32[256,256]{1,0:T(8,128)S(1)}, u32[]{:S(2)}, u32[]{:S(2)}) collective-permute-start(f32[256,256]{1,0:T(8,128)S(1)} %copy-done.2), channel_id=1, source_target_pairs={{0,24},{8,16},{16,8},{24,0},{1,25},{9,17},{17,9},{25,1},{2,26},{10... | collective-permute-start | bytes 786440 | tf_op jit(solution)/shard_map/ppermute | solution.py:354
  23.2 8.3 %collective-permute-start.5 = (f32[512,128]{1,0:T(8,128)S(1)}, f32[512,128]{1,0:T(8,128)S(1)}, u32[]{:S(2)}, u32[]{:S(2)}) collective-permute-start(f32[512,128]{1,0:T(8,128)S(1)} %copy-done.1), channel_id=1, source_target_pairs={{0,1},{1,0},{2,3},{3,2},{4,5},{5,4},{6,7},{7,6},{8,9},{9,8},{10,11... | collective-permute-start | bytes 786440 | tf_op jit(solution)/shard_map/ppermute | solution.py:348
  23.3 8.2 %collective-permute-start.7 = (f32[512,128]{1,0:T(8,128)S(1)}, f32[512,128]{1,0:T(8,128)S(1)}, u32[]{:S(2)}, u32[]{:S(2)}) collective-permute-start(f32[512,128]{1,0:T(8,128)S(1)} %collective-permute-done.6.refs_4_), channel_id=1, source_target_pairs={{0,1},{1,0},{2,3},{3,2},{4,5},{5,4},{6,7},{7,6},{8,9},{9,8},{10,11... | collective-permute-start | bytes 786440 | tf_op jit(solution)/shard_map/ppermute | solution.py:348
  23.8 8.7 %collective-permute-start.10 = (f32[512,128]{1,0:T(8,128)S(1)}, f32[512,128]{1,0:T(8,128)S(1)}, u32[]{:S(2)}, u32[]{:S(2)}) collective-permute-start(f32[512,128]{1,0:T(8,128)S(1)} %collective-permute-done.8.refs_6_.middle), channel_id=1, source_target_pairs={{0,1},{1,0},{2,3},{3,2},{4,5},{5,4},{6,7},{7,6},{8,9},{9,8},{10,11... | collective-permute-start | bytes 786440 | tf_op jit(solution)/shard_map/ppermute | solution.py:348
  27.8 4.8 %collective-permute-start.11 = (f32[448,128]{1,0:T(8,128)S(1)}, f32[448,128]{1,0:T(8,128)S(1)}, u32[]{:S(2)}, u32[]{:S(2)}) collective-permute-start(f32[448,128]{1,0:T(8,128)S(1)} %collective-permute-done.9.refs_7_), channel_id=1, source_target_pairs={{0,1},{1,0},{2,3},{3,2},{4,5},{5,4},{6,7},{7,6},{8,9},{9,8},{10,11... | collective-permute-start | bytes 688136 | tf_op jit(solution)/shard_map/ppermute | solution.py:348
  27.9 3.6 %copy-start = (f32[512,256]{1,0:T(8,128)S(1)}, f32[512,256]{1,0:T(8,128)}, u32[]{:S(2)}) copy-start(f32[512,256]{1,0:T(8,128)} %trail.1) | copy-start | bytes 1572868
  28.1 4.4 %collective-permute-start.12 = (f32[128,128]{1,0:T(8,128)S(1)}, f32[128,128]{1,0:T(8,128)S(1)}, u32[]{:S(2)}, u32[]{:S(2)}) collective-permute-start(f32[128,128]{1,0:T(8,128)S(1)} %get-tuple-element.50), channel_id=1, source_target_pairs={{2,0},{3,1},{4,6},{5,7},{0,2},{1,3},{6,4},{7,5},{10,8},{11,9},{12,... | collective-permute-start | bytes 196616 | tf_op jit(solution)/shard_map/ppermute | solution.py:348

commit v6 on v5

--- a/solution.py
+++ b/solution.py
@@ -123,9 +123,8 @@
     return kernel_call(first_kernel, "first_part", outs, (pivot,), scratch, 2)
 
 
-def second_kernel(g1h, g1l, u, l, d, shard, vh, vl, lowh, lowl, e, eh, el, head, uh, ul):
+def second_kernel(g1h, g1l, u, l, d, vh, vl, lowh, lowl, e, eh, el, uh, ul):
     n = u.shape[0]
-    head[...] = shard[pl.ds(0, head.shape[0]), :]
     g1, v, low, up = (g1h, g1l), (vh, vl), (lowh, lowl), (uh, ul)
     each(n, lambda cols, _: put(up, cols, u[:, cols]))
     each(n, lambda cols, _: put(v, cols, u[:, cols] + product(g1, up, cols)))
@@ -139,11 +138,19 @@
     each(n, residual)
 
 
-def second_part(g1, u, l, d, shard):
+def second_part(g1, u, l, d):
     n = u.shape[0]
+    outs = [half(n, n)] * 4 + [single(n, n)] + [half(n, n)] * 2
+    return kernel_call(second_kernel, "second_part", outs, (*g1, u, l, d), [pltpu.VMEM((n, n), BF16)] * 2, 2)
+
+
+def cut_kernel(shard, head):
+    head[...] = shard[pl.ds(0, head.shape[0]), :]
+
+
+def cut_part(shard):
     m, wide = shard.shape
-    outs = [half(n, n)] * 4 + [single(n, n)] + [half(n, n)] * 2 + [single(m - TAIL, wide)]
-    return kernel_call(second_kernel, "second_part", outs, (*g1, u, l, d, shard), [pltpu.VMEM((n, n), BF16)] * 2, 2)
+    return kernel_call(cut_kernel, "cut_part", [single(m - TAIL, wide)], (shard,), [], 0)[0]
 
 
 def third_kernel(e, eh, el, own, other, g2h, g2l, x, fh, fl, tails):
@@ -359,7 +366,8 @@
     rows = [row_panel] + [row(s) for s in range(1, n_row)]
     one_other = exchange(one)
     *g1, u, l, d = first_part(pivot)
-    vh, vl, lowh, lowl, *e, head = second_part(g1, u, l, d, one)
+    vh, vl, lowh, lowl, *e = second_part(g1, u, l, d)
+    head = cut_part(one)
     head = send(head, SEND_ENDS)
     *work, tails = third_part(e, one, one_other)
     tails = send(tails, SEND_ENDS)

time: 33.8 us -> 33.7 us (level)
  starting transfers between devices: 15.6 us -> 13.3 us
  waiting for transfers between devices: 6.03 us -> 8.24 us
    ppermute x3, waiting for transfers between devices: 0.21 us -> 3.77 us  [row(): return lax.ppermute(row_panel, 'row', [(i, i ^ s) for i in range(n_row)])]
    ppermute x10, starting transfers between devices: 10.2 us -> 7.73 us  [send(): return lax.ppermute(x, 'col', hops + swaps)]
    ppermute x10, waiting for transfers between devices: 5.82 us -> 4.47 us  [send(): return lax.ppermute(x, 'col', hops + swaps)]
    pallas_call x4 -> x5, Pallas kernels: 7.21 us -> 7.22 us  [kernel_call(): pl.pallas_call(body, out_shape=tuple(outs), in_specs=specs, out_specs=(VM...]
where the time goes in v6:
time: 33.7 us; the launch traced here: 33.5 us
  starting transfers between devices  13.3 us (39%)
  Pallas kernels  11.8 us (35%)
  waiting for transfers between devices  8.24 us (24%)
    ppermute x10, starting transfers between devices, send(): return lax.ppermute(x, 'col', hops + swaps)  7.73 us
    pallas_call x5, Pallas kernels, kernel_call(): pl.pallas_call(body, out_shape=tuple(outs), in_specs=specs, out_specs=(VM...  7.22 us
    ppermute x3, starting transfers between devices, row(): return lax.ppermute(row_panel, 'row', [(i, i ^ s) for i in range(n_row)])  5.56 us
    ppermute x10, waiting for transfers between devices, send(): return lax.ppermute(x, 'col', hops + swaps)  4.47 us
    ppermute x3, waiting for transfers between devices, row(): return lax.ppermute(row_panel, 'row', [(i, i ^ s) for i in range(n_row)])  3.77 us
    pallas_call x1, Pallas kernels, chain_part(): pl.pallas_call(chain_kernel, out_shape=(half(2 * n, width),) * 2, in_spec...  2.52 us
    pallas_call x1, Pallas kernels, last_part(): pl.pallas_call(functools.partial(last_kernel, blocks), out_shape=jax.Shap...  1.11 us
    pallas_call x1, Pallas kernels, update_part(): pl.pallas_call(functools.partial(update_kernel, tables), out_shape=jax.Sh...  0.98 us
  transfers between devices with their start and end apart: 13, of which 3 were waited for; matrix products, arithmetic and copies ran while one was open for 0% of the time, Pallas kernels for 32%

profile of v6, /device:TPU:0, one launch (start us, length us, event | category | flops | bytes accessed | tf_op | source)
XLA Modules:
  0.0 33.5 jit_solution(5659712254297301542)
XLA Ops:
  0.0 4.1 %collective-permute-start = (f32[512,128]{1,0:T(8,128)}, f32[512,128]{1,0:T(8,128)S(1)}, u32[]{:S(2)}, u32[]{:S(2)}) collective-permute-start(f32[512,128]{1,0:T(8,128)} %refs_0_.3), channel_id=1, source_target_pairs={{2,0},{3,1},{6,2},{7,3},{0,4},{1,5},{4,6},{5,7},{10,8},{11,9},{14,... | collective-permute-start | bytes 786440 | tf_op jit(solution)/shard_map/ppermute | solution.py:355
  4.1 1.5 %collective-permute-start.2 = (f32[256,256]{1,0:T(8,128)}, f32[256,256]{1,0:T(8,128)S(1)}, u32[]{:S(2)}, u32[]{:S(2)}) collective-permute-start(f32[256,256]{1,0:T(8,128)} %refs_0_.2), channel_id=1, source_target_pairs={{0,8},{8,0},{16,24},{24,16},{1,9},{9,1},{17,25},{25,17},{2,10},{10... | collective-permute-start | bytes 786440 | tf_op jit(solution)/shard_map/ppermute | solution.py:361
  5.6 1.5 %collective-permute-start.3 = (f32[256,256]{1,0:T(8,128)}, f32[256,256]{1,0:T(8,128)S(1)}, u32[]{:S(2)}, u32[]{:S(2)}) collective-permute-start(f32[256,256]{1,0:T(8,128)} %refs_0_.2), channel_id=1, source_target_pairs={{0,16},{8,24},{16,0},{24,8},{1,17},{9,25},{17,1},{25,9},{2,18},{10... | collective-permute-start | bytes 786440 | tf_op jit(solution)/shard_map/ppermute | solution.py:361
  7.1 0.0 collective-permute-start.6
  7.1 0.0 collective-permute-start.8
  7.1 4.0 %collective-permute-done.own.shard.refs_2_ = f32[512,128]{1,0:T(8,128)S(1)} collective-permute-done((f32[512,128]{1,0:T(8,128)}, f32[512,128]{1,0:T(8,128)S(1)}, u32[]{:S(2)}, u32[]{:S(2)}) %collective-permute-start) | collective-permute-done | bytes 262176 | tf_op jit(solution)/shard_map/ppermute | solution.py:355
  11.1 0.0 collective-permute-start.1
  11.1 3.2 %shard_map.46 = (bf16[512,512]{1,0:T(8,128)(2,1)S(1)}, bf16[512,512]{1,0:T(8,128)(2,1)S(1)}, f32[512,512]{1,0:T(8,128)S(1)}, f32[512,512]{1,0:T(8,128)S(1)}, f32[512,512]{1,0:T(8,128)S(1)}) custom-call(f32[1024,1024]{1,0:T(8,128)} %pivot.1), custom_call_target="tpu_custom_call" | custom-call | flops 1610612736 | bytes 4194304 | tf_op jit(solution)/shard_map/pallas_call | solution.py:98
  14.4 0.0 copy-start.2
  14.4 0.0 collective-permute-done.2.refs_1_
  14.4 2.3 %collective-permute-start.9 = (f32[448,128]{1,0:T(8,128)S(1)}, f32[448,128]{1,0:T(8,128)S(1)}, u32[]{:S(2)}, u32[]{:S(2)}) collective-permute-start(f32[448,128]{1,0:T(8,128)S(1)} %shard_map.50), channel_id=1, source_target_pairs={{2,0},{3,1},{4,6},{5,7},{0,2},{1,3},{6,4},{7,5},{10,8},{11,9},{12,... | collective-permute-start | bytes 688136 | tf_op jit(solution)/shard_map/ppermute | solution.py:355
  16.7 2.0 %shard_map.47 = (bf16[512,512]{1,0:T(8,128)(2,1)S(1)}, bf16[512,512]{1,0:T(8,128)(2,1)S(1)}, bf16[512,512]{1,0:T(8,128)(2,1)S(1)}, bf16[512,512]{1,0:T(8,128)(2,...) custom-call(bf16[512,512]{1,0:T(8,128)(2,1)S(1)} %get-tuple-element.27.g1h, ...), custom_call_target="tpu_custom_call" | custom-call | flops 1610612736 | bytes 4194304 | tf_op jit(solution)/shard_map/pallas_call | solution.py:98
  18.7 0.0 copy-start.1
  18.7 0.0 collective-permute-done.1.other.refs_3_
  18.7 0.0 copy-done.2
  18.8 2.6 %collective-permute-start.4 = (f32[256,256]{1,0:T(8,128)S(1)}, f32[256,256]{1,0:T(8,128)S(1)}, u32[]{:S(2)}, u32[]{:S(2)}) collective-permute-start(f32[256,256]{1,0:T(8,128)S(1)} %copy-done.2), channel_id=1, source_target_pairs={{0,24},{8,16},{16,8},{24,0},{1,25},{9,17},{17,9},{25,1},{2,26},{10... | collective-permute-start | bytes 786440 | tf_op jit(solution)/shard_map/ppermute | solution.py:361
  21.3 2.0 %shard_map.48 = (bf16[512,512]{1,0:T(8,128)(2,1)S(1)}, bf16[512,512]{1,0:T(8,128)(2,1)S(1)}, f32[512,512]{1,0:T(8,128)S(1)}, bf16[512,512]{1,0:T(8,128)(2,1)S(1)...) custom-call(f32[512,512]{1,0:T(8,128)S(1)} %get-tuple-element.38.e, bf16[512,512]{1,0:T(8,128)(2,1)S(1)} %get-tuple-element.36.eh, ...), custom_call_target="tpu_custom_call" | custom-call | flops 1610612736 | bytes 4194304 | tf_op jit(solution)/shard_map/pallas_call | solution.py:98
  23.3 0.0 collective-permute-done.3.refs_2_
  23.3 0.0 copy-done.1
  23.3 0.1 collective-permute-start.5
  23.4 0.0 collective-permute-done.6.refs_4_
  23.4 0.5 %collective-permute-start.7 = (f32[512,128]{1,0:T(8,128)S(1)}, f32[512,128]{1,0:T(8,128)S(1)}, u32[]{:S(2)}, u32[]{:S(2)}) collective-permute-start(f32[512,128]{1,0:T(8,128)S(1)} %collective-permute-done.6.refs_4_), channel_id=1, source_target_pairs={{0,1},{1,0},{2,3},{3,2},{4,5},{5,4},{6,7},{7,6},{8,9},{9,8},{10,11... | collective-permute-start | bytes 786440 | tf_op jit(solution)/shard_map/ppermute | solution.py:355
  23.9 0.0 collective-permute-done.8.refs_6_.middle
  23.9 0.1 collective-permute-start.10
  24.0 0.0 collective-permute-done.9.refs_7_
  24.0 0.4 %collective-permute-start.11 = (f32[448,128]{1,0:T(8,128)S(1)}, f32[448,128]{1,0:T(8,128)S(1)}, u32[]{:S(2)}, u32[]{:S(2)}) collective-permute-start(f32[448,128]{1,0:T(8,128)S(1)} %collective-permute-done.9.refs_7_), channel_id=1, source_target_pairs={{0,1},{1,0},{2,3},{3,2},{4,5},{5,4},{6,7},{7,6},{8,9},{9,8},{10,11... | collective-permute-start | bytes 688136 | tf_op jit(solution)/shard_map/ppermute | solution.py:355
  24.4 0.0 copy-start
  24.4 3.8 %collective-permute-done.4.refs_3_ = f32[256,256]{1,0:T(8,128)S(1)} collective-permute-done((f32[256,256]{1,0:T(8,128)S(1)}, f32[256,256]{1,0:T(8,128)S(1)}, u32[]{:S(2)}, u32[]{:S(2)}) %collective-permute-start.4) | collective-permute-done | bytes 262176 | tf_op jit(solution)/shard_map/ppermute | solution.py:361
  28.2 0.3 collective-permute-start.12
  28.4 2.5 %chain_part.1 = (bf16[1024,256]{1,0:T(8,128)(2,1)S(1)}, bf16[1024,256]{1,0:T(8,128)(2,1)S(1)}) custom-call(bf16[512,512]{1,0:T(8,128)(2,1)S(1)} %get-tuple-element.27.g1h, bf16[512,512]{1,0:T(8,128)(2,1)S(1)} %get-tuple-element.28.g1l, bf16[512,512]{1,0:T(8,128)(2,1)S(1)} %get-tuple-element.32.vh, bf16[512,512]{1,0:T(8,128)(2,1)S(1)} %get-tuple-element.33.vl, ...), custom_call_target="tpu_custom_call" | custom-call | flops 1610612736 | bytes 6291456 | tf_op jit(solution)/shard_map/chain_part/pallas_call | solution.py:238
  31.0 0.0 collective-permute-done.5.refs_1_
  31.0 0.0 collective-permute-done.7.refs_5_
  31.0 0.0 copy-done
  31.0 1.0 %update_part.1.part = f32[512,256]{1,0:T(8,128)S(1)} custom-call(f32[512,256]{1,0:T(8,128)S(1)} %copy-done, bf16[1024,256]{1,0:T(8,128)(2,1)S(1)} %get-tuple-element.46.yh, bf16[1024,256]{1,0:T(8,128)(2,1)S(1)} %get-tuple-element.47.yl, f32[512,128]{1,0:T(8,128)S(1)} %copy-done.1, f32[512,128]{1,0:T(8,128)S(1)} %collective-permute-done.5.refs_1_, ...), custom_call_target="tpu_custom_call" | custom-call | flops 805306368 | bytes 3145728 | tf_op jit(solution)/shard_map/update_part/pallas_call | solution.py:302
  32.0 0.0 collective-permute-done.10.middle_other
  32.0 0.4 %collective-permute-done.12.tails = f32[128,128]{1,0:T(8,128)S(1)} collective-permute-done((f32[128,128]{1,0:T(8,128)S(1)}, f32[128,128]{1,0:T(8,128)S(1)}, u32[]{:S(2)}, u32[]{:S(2)}) %collective-permute-start.12) | collective-permute-done | bytes 65568 | tf_op jit(solution)/shard_map/ppermute | solution.py:355
  32.4 0.0 collective-permute-done.11.head_other
  32.4 1.1 %last_part.1 = f32[512,256]{1,0:T(8,128)} custom-call(f32[512,256]{1,0:T(8,128)S(1)} %update_part.1.part, bf16[1024,256]{1,0:T(8,128)(2,1)S(1)} %get-tuple-element.46.yh, bf16[1024,256]{1,0:T(8,128)(2,1)S(1)} %get-tuple-element.47.yl, f32[512,128]{1,0:T(8,128)S(1)} %collective-permute-done.8.refs_6_.middle, ...), custom_call_target="tpu_custom_call" | custom-call | flops 100663296 | bytes 1572864 | tf_op jit(solution)/shard_map/last_part/pallas_call | solution.py:336
  (2 shorter events, 0.0 us)
Async XLA Ops:
  0.0 11.1 %collective-permute-start = (f32[512,128]{1,0:T(8,128)}, f32[512,128]{1,0:T(8,128)S(1)}, u32[]{:S(2)}, u32[]{:S(2)}) collective-permute-start(f32[512,128]{1,0:T(8,128)} %refs_0_.3), channel_id=1, source_target_pairs={{2,0},{3,1},{6,2},{7,3},{0,4},{1,5},{4,6},{5,7},{10,8},{11,9},{14,... | collective-permute-start | bytes 786440 | tf_op jit(solution)/shard_map/ppermute | solution.py:355
  4.1 10.3 %collective-permute-start.2 = (f32[256,256]{1,0:T(8,128)}, f32[256,256]{1,0:T(8,128)S(1)}, u32[]{:S(2)}, u32[]{:S(2)}) collective-permute-start(f32[256,256]{1,0:T(8,128)} %refs_0_.2), channel_id=1, source_target_pairs={{0,8},{8,0},{16,24},{24,16},{1,9},{9,1},{17,25},{25,17},{2,10},{10... | collective-permute-start | bytes 786440 | tf_op jit(solution)/shard_map/ppermute | solution.py:361
  5.6 17.7 %collective-permute-start.3 = (f32[256,256]{1,0:T(8,128)}, f32[256,256]{1,0:T(8,128)S(1)}, u32[]{:S(2)}, u32[]{:S(2)}) collective-permute-start(f32[256,256]{1,0:T(8,128)} %refs_0_.2), channel_id=1, source_target_pairs={{0,16},{8,24},{16,0},{24,8},{1,17},{9,25},{17,1},{25,9},{2,18},{10... | collective-permute-start | bytes 786440 | tf_op jit(solution)/shard_map/ppermute | solution.py:361
  7.1 16.3 %collective-permute-start.6 = (f32[512,128]{1,0:T(8,128)}, f32[512,128]{1,0:T(8,128)S(1)}, u32[]{:S(2)}, u32[]{:S(2)}) collective-permute-start(f32[512,128]{1,0:T(8,128)} %refs_0_.3), channel_id=1, source_target_pairs={{4,0},{5,1},{0,2},{1,3},{6,4},{7,5},{2,6},{3,7},{12,8},{13,9},{8,1... | collective-permute-start | bytes 786440 | tf_op jit(solution)/shard_map/ppermute | solution.py:355
  7.1 16.8 %collective-permute-start.8 = (f32[512,128]{1,0:T(8,128)}, f32[512,128]{1,0:T(8,128)S(1)}, u32[]{:S(2)}, u32[]{:S(2)}) collective-permute-start(f32[512,128]{1,0:T(8,128)} %refs_0_.3), channel_id=1, source_target_pairs={{2,4},{3,5},{4,2},{5,3},{0,1},{1,0},{6,7},{7,6},{10,12},{11,13},{1... | collective-permute-start | bytes 786440 | tf_op jit(solution)/shard_map/ppermute | solution.py:355
  11.1 7.6 %collective-permute-start.1 = (f32[512,128]{1,0:T(8,128)S(1)}, f32[512,128]{1,0:T(8,128)S(1)}, u32[]{:S(2)}, u32[]{:S(2)}) collective-permute-start(f32[512,128]{1,0:T(8,128)S(1)} %collective-permute-done.own.shard.refs_2_), channel_id=1, source_target_pairs={{0,1},{1,0},{2,3},{3,2},{4,5},{5,4},{6,7},{7,6},{8,9},{9,8},{10,11... | collective-permute-start | bytes 786440 | tf_op jit(solution)/shard_map/ppermute | solution.py:355
  14.4 4.4 %copy-start.2 = (f32[256,256]{1,0:T(8,128)S(1)}, f32[256,256]{1,0:T(8,128)}, u32[]{:S(2)}) copy-start(f32[256,256]{1,0:T(8,128)} %refs_0_.2) | copy-start | bytes 786436
  14.4 9.6 %collective-permute-start.9 = (f32[448,128]{1,0:T(8,128)S(1)}, f32[448,128]{1,0:T(8,128)S(1)}, u32[]{:S(2)}, u32[]{:S(2)}) collective-permute-start(f32[448,128]{1,0:T(8,128)S(1)} %shard_map.50), channel_id=1, source_target_pairs={{2,0},{3,1},{4,6},{5,7},{0,2},{1,3},{6,4},{7,5},{10,8},{11,9},{12,... | collective-permute-start | bytes 688136 | tf_op jit(solution)/shard_map/ppermute | solution.py:355
  18.7 4.6 %copy-start.1 = (f32[512,128]{1,0:T(8,128)S(1)}, f32[512,128]{1,0:T(8,128)}, u32[]{:S(2)}) copy-start(f32[512,128]{1,0:T(8,128)} %refs_0_.3) | copy-start | bytes 786436
  18.8 9.4 %collective-permute-start.4 = (f32[256,256]{1,0:T(8,128)S(1)}, f32[256,256]{1,0:T(8,128)S(1)}, u32[]{:S(2)}, u32[]{:S(2)}) collective-permute-start(f32[256,256]{1,0:T(8,128)S(1)} %copy-done.2), channel_id=1, source_target_pairs={{0,24},{8,16},{16,8},{24,0},{1,25},{9,17},{17,9},{25,1},{2,26},{10... | collective-permute-start | bytes 786440 | tf_op jit(solution)/shard_map/ppermute | solution.py:361
  23.3 7.7 %collective-permute-start.5 = (f32[512,128]{1,0:T(8,128)S(1)}, f32[512,128]{1,0:T(8,128)S(1)}, u32[]{:S(2)}, u32[]{:S(2)}) collective-permute-start(f32[512,128]{1,0:T(8,128)S(1)} %copy-done.1), channel_id=1, source_target_pairs={{0,1},{1,0},{2,3},{3,2},{4,5},{5,4},{6,7},{7,6},{8,9},{9,8},{10,11... | collective-permute-start | bytes 786440 | tf_op jit(solution)/shard_map/ppermute | solution.py:355
  23.4 7.6 %collective-permute-start.7 = (f32[512,128]{1,0:T(8,128)S(1)}, f32[512,128]{1,0:T(8,128)S(1)}, u32[]{:S(2)}, u32[]{:S(2)}) collective-permute-start(f32[512,128]{1,0:T(8,128)S(1)} %collective-permute-done.6.refs_4_), channel_id=1, source_target_pairs={{0,1},{1,0},{2,3},{3,2},{4,5},{5,4},{6,7},{7,6},{8,9},{9,8},{10,11... | collective-permute-start | bytes 786440 | tf_op jit(solution)/shard_map/ppermute | solution.py:355
  23.9 8.1 %collective-permute-start.10 = (f32[512,128]{1,0:T(8,128)S(1)}, f32[512,128]{1,0:T(8,128)S(1)}, u32[]{:S(2)}, u32[]{:S(2)}) collective-permute-start(f32[512,128]{1,0:T(8,128)S(1)} %collective-permute-done.8.refs_6_.middle), channel_id=1, source_target_pairs={{0,1},{1,0},{2,3},{3,2},{4,5},{5,4},{6,7},{7,6},{8,9},{9,8},{10,11... | collective-permute-start | bytes 786440 | tf_op jit(solution)/shard_map/ppermute | solution.py:355
  24.0 8.5 %collective-permute-start.11 = (f32[448,128]{1,0:T(8,128)S(1)}, f32[448,128]{1,0:T(8,128)S(1)}, u32[]{:S(2)}, u32[]{:S(2)}) collective-permute-start(f32[448,128]{1,0:T(8,128)S(1)} %collective-permute-done.9.refs_7_), channel_id=1, source_target_pairs={{0,1},{1,0},{2,3},{3,2},{4,5},{5,4},{6,7},{7,6},{8,9},{9,8},{10,11... | collective-permute-start | bytes 688136 | tf_op jit(solution)/shard_map/ppermute | solution.py:355
  24.4 6.6 %copy-start = (f32[512,256]{1,0:T(8,128)S(1)}, f32[512,256]{1,0:T(8,128)}, u32[]{:S(2)}) copy-start(f32[512,256]{1,0:T(8,128)} %trail.1) | copy-start | bytes 1572868
  28.2 4.3 %collective-permute-start.12 = (f32[128,128]{1,0:T(8,128)S(1)}, f32[128,128]{1,0:T(8,128)S(1)}, u32[]{:S(2)}, u32[]{:S(2)}) collective-permute-start(f32[128,128]{1,0:T(8,128)S(1)} %get-tuple-element.48), channel_id=1, source_target_pairs={{2,0},{3,1},{4,6},{5,7},{0,2},{1,3},{6,4},{7,5},{10,8},{11,9},{12,... | collective-permute-start | bytes 196616 | tf_op jit(solution)/shard_map/ppermute | solution.py:355
